TPU v7x, 32 devices: a whole 2x2x4 slice. The times are simulated.
32 devices in a mesh: band: 4 (over z), strip: 8 (over y, x, core).
Axes of the slice: x: 2, y: 2, z: 4, core: 2. Of those that a mesh axis runs over, the one named last changes fastest.
Arguments:
- first_scene: bfloat16 [2048, 4096], P('band', 'strip'), may hold values from -6 to 6
- second_scene: bfloat16 [2048, 4096], P('band', 'strip'), may hold values from -6 to 6
- owner_strip: int32 [4, 8, 16, 1], P('band', 'strip'), may hold values from 0 to 7; in each aligned block of 16 rows (0 to 15, 16 to 31, ..., all dimensions but the last counted through in order) at most 4 rows name the same one
- target_tile: int32 [4, 8, 16], P('band', 'strip'), may hold values from 0 to 15
- offsets: int32 [4, 8, 16, 2], P('band', 'strip'), may hold values from -32 to 32
- valid_mask: int32 [4, 8, 16], P('band', 'strip'), may hold values 0 or 1
Outputs:
- consistency: float32 [4, 8, 16, 4096], P('band', 'strip')
Inputs may be any that keep to these rules, and one draw needn't show every extreme that they name: `owner_strip`: among the 16 patches of one device at most 4 name the same owner strip, and in every draw some device has 4 patches naming one strip.
All inputs are finite; a program needn't handle non-finite values. No bound on the sum of `valid_mask` on one device may be relied on, other than what follows from the above.
Results may differ from a plain program's by a relative error of at most 0.0003.
Values may be sent and summed in bfloat16 or wider, within the bound.
A program may use at most 128 MiB of HBM per device.

v0:
```python
import functools

import jax
import jax.numpy as jnp
from jax import lax
from jax.experimental import pallas as pl
from jax.experimental.pallas import tpu as pltpu
from jax.sharding import PartitionSpec as P

PATCH_SIDE = 128
SHIFTS = 64
SEARCH = 192
WIDE = 256
LANES = 128
HALO = 64
EPSILON = 1e-05
GROUPS = 16
STEP = SEARCH // GROUPS
CHUNK = 16
HIGHEST = lax.Precision.HIGHEST
NT = (((1,), (1,)), ((), ()))


def iota(shape, dim):
    return lax.broadcasted_iota(jnp.int32, shape, dim)


def onehot(mask):
    return jnp.where(mask, 1.0, 0.0).astype(jnp.bfloat16)


def cut(raw, row_start, col_start, row_inner, col_inner, low, high):
    row_id = iota((SEARCH, WIDE), 0)
    source = row_start + STEP * (GROUPS - 1 - row_id % GROUPS) + row_id // GROUPS
    take_rows = onehot(iota((SEARCH, WIDE), 1) == source)
    inner_id = iota((WIDE + 16, WIDE), 0) - (SHIFTS - 1)
    inside = (inner_id >= 0) & (inner_id < PATCH_SIDE)
    take_inner = onehot(
        (iota((WIDE + 16, WIDE), 1) == row_start + row_inner + inner_id) & inside
    )
    rows = jnp.dot(
        jnp.concatenate([take_rows, take_inner], axis=0), raw, preferred_element_type=jnp.float32
    ).astype(jnp.bfloat16)
    from_col = iota((3 * LANES, WIDE), 0)
    to_col = iota((3 * LANES, WIDE), 1)
    real = (from_col >= low) & (from_col < high)
    take_cols = onehot((from_col == to_col + col_start) & (to_col < SEARCH) & real)
    window = jnp.dot(rows[:SEARCH], take_cols, preferred_element_type=jnp.float32)
    from_col = iota((3 * LANES, LANES), 0)
    real = (from_col >= low) & (from_col < high)
    take_cols = onehot(
        (from_col == iota((3 * LANES, LANES), 1) + col_start + col_inner) & real
    )
    inner = jnp.dot(rows[SEARCH:], take_cols, preferred_element_type=jnp.float32)
    return window, inner


def correlate(window, inner, inner_ref, weight_ref, shift_ref, reverse):
    inner_ref[...] = inner
    for i in range(STEP):
        weight_ref[:, i * LANES : (i + 1) * LANES] = inner_ref[i : i + WIDE, :].astype(jnp.bfloat16)
    count = PATCH_SIDE * PATCH_SIDE
    patch = inner_ref[SHIFTS - 1 : SHIFTS - 1 + PATCH_SIDE, :]
    mean = jnp.sum(patch) / count
    centered = patch - mean
    gain = lax.rsqrt(jnp.full((1, LANES), jnp.sum(centered * centered) / count + EPSILON))

    lane = iota((SEARCH, LANES), 1)
    left, right = window[:, :LANES], window[:, LANES:]
    parts = []
    for first in range(0, SHIFTS, CHUNK):
        for slot in range(first, first + CHUNK):
            shift = SHIFTS - 1 - slot if reverse else slot
            if shift:
                moved = pltpu.roll(jnp.where(lane < shift, right, left), LANES - shift, 1)
            else:
                moved = left
            moved = moved.astype(jnp.bfloat16)
            for i in range(STEP):
                shift_ref[slot * GROUPS : (slot + 1) * GROUPS, i * LANES : (i + 1) * LANES] = moved[
                    i * GROUPS : (i + 1) * GROUPS
                ]
        product = lax.dot_general(
            shift_ref[first * GROUPS : (first + CHUNK) * GROUPS, :],
            weight_ref[...],
            NT,
            preferred_element_type=jnp.float32,
        )
        for k in range(CHUNK):
            rows = product[k * GROUPS : (k + 1) * GROUPS]
            half = GROUPS // 2
            rows = rows[:half] + pltpu.roll(rows[half:], STEP * half, 1)
            skewed = pltpu.roll(rows, 0, 1, stride=STEP, stride_axis=0)
            parts.append(jnp.sum(skewed, axis=0, keepdims=True))
    raw = jnp.concatenate(parts, axis=0)
    raw = pltpu.roll(raw, WIDE - STEP * (GROUPS - 1), 1)[:, :LANES]

    slot = iota((SHIFTS, WIDE), 0)
    v = SHIFTS - 1 - slot if reverse else slot
    col = iota((SHIFTS, WIDE), 1)
    across = lax.dot_general(
        onehot((col >= v) & (col < v + PATCH_SIDE)),
        window.astype(jnp.bfloat16),
        NT,
        preferred_element_type=jnp.float32,
    )
    row_id = iota((SEARCH, LANES), 0)
    row = STEP * (GROUPS - 1 - row_id % GROUPS) + row_id // GROUPS
    u = SHIFTS - 1 - lane
    down = jnp.where((row >= u) & (row < u + PATCH_SIDE), 1.0, 0.0)
    sums = jnp.dot(across, down, precision=HIGHEST, preferred_element_type=jnp.float32)
    return gain * (raw - mean * sums)


def kernel(per_row, tiles, owner, tile, offset, valid, *refs):
    first, second = refs[:6], refs[6:12]
    out_ref, inner_ref, weight_ref, shift_ref = refs[12:]
    k = pl.program_id(0)
    middle = SHIFTS // 2

    def gathered(blocks):
        return jnp.concatenate(
            [
                jnp.concatenate([blocks[3 * r + c][...].reshape(LANES, LANES) for c in range(3)], axis=1)
                for r in range(2)
            ],
            axis=0,
        )

    around = cut(
        gathered(first), HALO - middle + 1, LANES - middle + 1, middle - 1, middle - 1, 0, 3 * LANES
    )
    place = owner[k] * per_row + tile[k] % per_row
    low = jnp.where(place == 0, LANES, 0)
    high = jnp.where(place == tiles - 1, 2 * LANES, 3 * LANES)
    search = cut(
        gathered(second),
        HALO - middle + offset[2 * k],
        LANES - middle + offset[2 * k + 1],
        middle,
        middle,
        low,
        high,
    )
    ahead = correlate(search[0], around[1], inner_ref, weight_ref, shift_ref, False)
    behind = correlate(around[0], search[1], inner_ref, weight_ref, shift_ref, True)
    lane = iota((SHIFTS, LANES), 1)
    both = jnp.where(lane < SHIFTS, ahead, pltpu.roll(behind, SHIFTS, 1))
    u = iota((SHIFTS, LANES), 0)
    pick = jnp.where((lane == SHIFTS - 1 - u) | (lane == SHIFTS + u), 1.0, 0.0)
    surface = lax.dot_general(
        pick, both, NT, precision=HIGHEST, preferred_element_type=jnp.float32
    )
    scale = valid[k].astype(jnp.float32) / (2.0 * PATCH_SIDE)
    out_ref[0] = surface * scale


def surfaces(first, gathered, owner, tile, offset, valid):
    strips = gathered.shape[0]
    per_row = gathered.shape[2] // LANES
    tiles = strips * per_row
    patch_count = owner.shape[0]

    def first_spec(r, c):
        return pl.BlockSpec((LANES, LANES), lambda k, *_: (k // per_row + r, k % per_row + c))

    def second_spec(r, c):
        def index(k, owner, tile, offset, valid):
            place = owner[k] * per_row + tile[k] % per_row + (c - 1)
            place = jnp.minimum(jnp.maximum(place, 0), tiles - 1)
            return (place // per_row, tile[k] // per_row + r, place % per_row)

        return pl.BlockSpec((1, LANES, LANES), index)

    cells = [(r, c) for r in range(2) for c in range(3)]
    return pl.pallas_call(
        functools.partial(kernel, per_row, tiles),
        out_shape=jax.ShapeDtypeStruct((patch_count, SHIFTS, SHIFTS), jnp.float32),
        grid_spec=pltpu.PrefetchScalarGridSpec(
            num_scalar_prefetch=4,
            grid=(patch_count,),
            in_specs=[first_spec(*cell) for cell in cells] + [second_spec(*cell) for cell in cells],
            out_specs=pl.BlockSpec((1, SHIFTS, SHIFTS), lambda k, *_: (k, 0, 0)),
            scratch_shapes=[
                pltpu.VMEM((WIDE + 16, LANES), jnp.float32),
                pltpu.VMEM((WIDE, STEP * LANES), jnp.bfloat16),
                pltpu.VMEM((SHIFTS * GROUPS, STEP * LANES), jnp.bfloat16),
            ],
        ),
    )(owner, tile, offset, valid, *([first] * 6), *([gathered] * 6))


def both_ways(axis, tail, head):
    count = lax.axis_size(axis)
    before = lax.ppermute(tail, axis, [(i, i + 1) for i in range(count - 1)])
    after = lax.ppermute(head, axis, [(i + 1, i) for i in range(count - 1)])
    return before, after


def on_device(first_scene, second_scene, owner_strip, target_tile, offsets, valid_mask):
    per_row = first_scene.shape[1] // PATCH_SIDE
    patch_count = first_scene.shape[0] // PATCH_SIDE * per_row
    above, below = both_ways(
        "band",
        jnp.concatenate([first_scene[-HALO:], second_scene[-HALO:]], axis=0),
        jnp.concatenate([first_scene[:HALO], second_scene[:HALO]], axis=0),
    )
    second = jnp.concatenate([above[HALO:], second_scene, below[HALO:]], axis=0)
    gathered = lax.all_gather(second, "strip", axis=0)
    first = jnp.concatenate([above[:HALO], first_scene, below[:HALO]], axis=0)
    before, after = both_ways("strip", first[:, -LANES:], first[:, :LANES])
    first = jnp.concatenate([before, first, after], axis=1)
    result = surfaces(
        first,
        gathered,
        owner_strip.reshape(patch_count),
        target_tile.reshape(patch_count),
        offsets.reshape(2 * patch_count),
        valid_mask.reshape(patch_count),
    )
    return result.reshape(1, 1, patch_count, SHIFTS * SHIFTS)


def solution(mesh):
    return jax.shard_map(
        on_device,
        mesh=mesh,
        in_specs=(
            P("band", "strip"),
            P("band", "strip"),
            P("band", "strip", None, None),
            P("band", "strip", None),
            P("band", "strip", None, None),
            P("band", "strip", None),
        ),
        out_specs=P("band", "strip", None, None),
        check_vma=False,
    )
```

profile of v0, /device:TPU:0, one launch (start us, length us, event | category | flops | bytes accessed | tf_op | source)
XLA Modules:
  0.0 147.9 jit_solution(15760654538046368536)
XLA Ops:
  6.5 0.0 copy-start
  6.5 0.0 all-gather.3.cloned.1.call-start
  6.5 1.0 fusion
  7.6 0.0 copy-start.1
  7.6 5.0 %collective-permute-start = (bf16[128,512]{1,0:T(8,128)(2,1)S(1)}, bf16[128,512]{1,0:T(8,128)(2,1)S(1)}, u32[]{:S(2)}, u32[]{:S(2)}) collective-permute-start(bf16[128,512]{1,0:T(8,128)(2,1)S(1)} %pad_maximum_fusion.5), channel_id=1, source_target_pairs={{0,8},{8,16},{16,24},{1,9},{9,17},{17,25},{2,10},{10,18},{18,26},{... | collective-permute-start | bytes 393224 | tf_op jit(solution)/shard_map/ppermute | solution.py:195
  12.6 1.3 collective-permute-start.1
  13.9 1.4 collective-permute-done
  15.3 4.1 %collective-permute-done.1 = bf16[128,512]{1,0:T(8,128)(2,1)S(1)} collective-permute-done((bf16[128,512]{1,0:T(8,128)(2,1)S(1)}, bf16[128,512]{1,0:T(8,128)(2,1)S(1)}, u32[]{:S(2)}, u32[]{:S(2)}) %collective-permute-start.1) | collective-permute-done | bytes 131104 | tf_op jit(solution)/shard_map/ppermute | solution.py:196
  19.4 1.9 %pad_maximum_fusion.1 = bf16[640,512]{1,0:T(8,128)(2,1)} fusion(bf16[64,512]{1,0:T(8,128)(2,1)S(1)} %get-tuple-element.13, bf16[512,512]{1,0:T(8,128)(2,1)} %param.7, bf16[64,512]{1,0:T(8,128)(2,1)S(1)} %get-tuple-element.11), kind=kLoop, calls=%fused_computation.1 | loop fusion | flops 1966080 | bytes 1310720 | tf_op jit(solution)/shard_map/concatenate | solution.py:208
  21.4 0.0 all-gather.3.cloned.1.call-update
  21.4 0.0 copy-done
  21.4 1.3 collective-permute-start.2
  22.8 1.3 collective-permute-start.3
  24.1 0.0 copy-done.1
  24.1 0.1 copy.8
  24.2 0.6 reshape.17.offset
  24.8 0.0 collective-permute-done.2
  24.8 3.0 %collective-permute-done.3 = bf16[640,128]{1,0:T(8,128)(2,1)S(1)} collective-permute-done((bf16[640,128]{1,0:T(8,128)(2,1)S(1)}, bf16[640,128]{1,0:T(8,128)(2,1)S(1)}, u32[]{:S(2)}, u32[]{:S(2)}) %collective-permute-start.3) | collective-permute-done | bytes 163872 | tf_op jit(solution)/shard_map/ppermute | solution.py:196
  27.8 1.1 pad_maximum_fusion.refs_0_.refs_1_.refs_2_.refs_3_.refs_4_.refs_5_
  28.8 33.9 %all-gather.3.cloned.1.call-done = bf16[5120,512]{1,0:T(8,128)(2,1)} async-done(((bf16[640,512]{1,0:T(8,128)(2,1)}), bf16[5120,512]{1,0:T(8,128)(2,1)}) %all-gather.3.cloned.1.call-update) | async-done | bytes 5242896 | tf_op jit(solution)/shard_map/all_gather | solution.py:209
  62.8 76.4 %shard_map.64 = f32[16,64,64]{2,1,0:T(8,128)} custom-call(s32[16]{0:T(128)} %bitcast.12, s32[16]{0:T(128)} %bitcast.13, s32[32]{0:T(128)} %reshape.17.offset, s32[16]{0:T(128)} %bitcast.14, bf16[640,768]{1,0:T(8,128)(2,1)} %pad_maximum_fusion.refs_0_.refs_1_.refs_2_.refs_3_.refs_4_.refs_5_, ...), custom_call_target="tpu_custom_call" | custom-call | tf_op jit(solution)/shard_map/pallas_call | solution.py:176
  139.2 1.9 %reshape.19 = f32[1,1,16,4096]{3,2,1,0:T(8,128)} reshape(f32[16,64,64]{2,1,0:T(8,128)} %shard_map.64) | data formatting | bytes 524288 | tf_op jit(solution)/shard_map/reshape | solution.py:221
  (5 shorter events, 0.1 us)
Async XLA Ops:
  6.5 14.9 %copy-start = (bf16[512,512]{1,0:T(8,128)(2,1)S(1)}, bf16[512,512]{1,0:T(8,128)(2,1)}, u32[]{:S(2)}) copy-start(bf16[512,512]{1,0:T(8,128)(2,1)} %param.6) | copy-start | bytes 1572868
  6.5 56.2 %all-gather.3.cloned.1.call-start = ((), (), s32[]{:S(2)}) async-start(), calls=%async_computation | async-start | bytes 5898240 | tf_op jit(solution)/shard_map/all_gather | solution.py:209
  7.6 16.5 %copy-start.1 = (s32[1,1,16,2]{2,3,1,0:T(2,128)S(1)}, s32[1,1,16,2]{2,3,1,0:T(2,128)}, u32[]{:S(2)}) copy-start(s32[1,1,16,2]{2,3,1,0:T(2,128)} %param.10) | copy-start | bytes 388
  7.6 7.7 %collective-permute-start = (bf16[128,512]{1,0:T(8,128)(2,1)S(1)}, bf16[128,512]{1,0:T(8,128)(2,1)S(1)}, u32[]{:S(2)}, u32[]{:S(2)}) collective-permute-start(bf16[128,512]{1,0:T(8,128)(2,1)S(1)} %pad_maximum_fusion.5), channel_id=1, source_target_pairs={{0,8},{8,16},{16,24},{1,9},{9,17},{17,25},{2,10},{10,18},{18,26},{... | collective-permute-start | bytes 393224 | tf_op jit(solution)/shard_map/ppermute | solution.py:195
  12.6 6.9 %collective-permute-start.1 = (bf16[128,512]{1,0:T(8,128)(2,1)S(1)}, bf16[128,512]{1,0:T(8,128)(2,1)S(1)}, u32[]{:S(2)}, u32[]{:S(2)}) collective-permute-start(bf16[128,512]{1,0:T(8,128)(2,1)S(1)} %pad_maximum_fusion.6), channel_id=1, source_target_pairs={{8,0},{16,8},{24,16},{9,1},{17,9},{25,17},{10,2},{18,10},{26,18},{... | collective-permute-start | bytes 393224 | tf_op jit(solution)/shard_map/ppermute | solution.py:196
  21.4 3.3 %collective-permute-start.2 = (bf16[640,128]{1,0:T(8,128)(2,1)S(1)}, bf16[640,128]{1,0:T(8,128)(2,1)S(1)}, u32[]{:S(2)}, u32[]{:S(2)}) collective-permute-start(bf16[640,128]{1,0:T(8,128)(2,1)S(1)} %get-tuple-element.5), channel_id=1, source_target_pairs={{0,1},{1,2},{2,3},{3,4},{4,5},{5,6},{6,7},{8,9},{9,10},{10,11},{11... | collective-permute-start | bytes 491528 | tf_op jit(solution)/shard_map/ppermute | solution.py:195
  22.8 5.0 %collective-permute-start.3 = (bf16[640,128]{1,0:T(8,128)(2,1)S(1)}, bf16[640,128]{1,0:T(8,128)(2,1)S(1)}, u32[]{:S(2)}, u32[]{:S(2)}) collective-permute-start(bf16[640,128]{1,0:T(8,128)(2,1)S(1)} %get-tuple-element.6), channel_id=1, source_target_pairs={{1,0},{2,1},{3,2},{4,3},{5,4},{6,5},{7,6},{9,8},{10,9},{11,10},{12... | collective-permute-start | bytes 491528 | tf_op jit(solution)/shard_map/ppermute | solution.py:196
Sparse Core Ops, SparseCore 0:
  21.5 41.2 all-gather.2
where the time goes:
time: 148 us
  Pallas kernels  76.4 us (52%)
  waiting for transfers between devices  42.5 us (29%)
  between operations  13.5 us (9%)
  starting transfers between devices  8.85 us (6%)
  local copies, waits for them, and re-layouts  3.65 us (2%)
  other arithmetic  3.05 us (2%)
    pallas_call x1, Pallas kernels, surfaces(): pl.pallas_call(functools.partial(kernel, per_row, tiles), out_shape=jax.S...  76.4 us
    all_gather x1, waiting for transfers between devices, on_device(): gathered = lax.all_gather(second, 'strip', axis=0)  33.9 us
    ppermute x2, waiting for transfers between devices, both_ways(): after = lax.ppermute(head, axis, [(i + 1, i) for i in range(count - 1)])  7.14 us
    ppermute x2, starting transfers between devices, both_ways(): before = lax.ppermute(tail, axis, [(i, i + 1) for i in range(count - 1)])  6.26 us
  transfers between devices with their start and end apart: 5, of which 4 were waited for; matrix products, arithmetic and copies ran while one was open for 1% of the time, Pallas kernels for 0%

commit v1 on v0

v1 whole, which is shorter than its diff:
```python
import functools

import jax
import jax.numpy as jnp
import numpy as np
from jax import lax
from jax.experimental import pallas as pl
from jax.experimental.pallas import tpu as pltpu
from jax.sharding import PartitionSpec as P

PATCH_SIDE = 128
SHIFTS = 64
EDGE = SHIFTS // 2
SEARCH = PATCH_SIDE + SHIFTS
CYCLE = SEARCH - 1
BINS = (CYCLE + 1) // 2
LANES = 128
WIDE = 2 * LANES
HALO = 64
ROWS = SEARCH + 16
EPSILON = 1e-05
F32 = jnp.float32
BF16 = jnp.bfloat16


def two(x):
    high = x.astype(BF16)
    return high, (x - high.astype(F32)).astype(BF16)


def two_np(x):
    high = x.astype(jnp.bfloat16)
    low = (x - high.astype(np.float64)).astype(jnp.bfloat16)
    return high, low


def tables():
    angle = 2 * np.pi / CYCLE
    freq = np.arange(BINS)

    def across(place, real):
        out = np.zeros((LANES, WIDE))
        phase = angle * place[:, None] * freq[None, :]
        out[:, :BINS] = np.cos(phase) * real[:, None]
        out[:, LANES : LANES + BINS] = np.sin(phase) * real[:, None]
        return out

    def down(place, real):
        phase = angle * place[None, :] * freq[:, None]
        return np.concatenate([np.cos(phase), np.sin(phase)], axis=0) * real[None, :]

    lane = np.arange(LANES)
    edge_place = np.where(lane < LANES // 2, PATCH_SIDE + lane, lane - LANES)
    row = np.arange(SEARCH) - EDGE
    made = {}
    sums = []
    inner = across(lane, np.ones(LANES))
    high, low = two_np(inner)
    made["inner"] = np.concatenate([high, low], axis=0)
    sums.append((high.astype(np.float64) + low.astype(np.float64)).sum(0))
    high, low = two_np(down(row[EDGE : EDGE + PATCH_SIDE], np.ones(PATCH_SIDE)))
    made["down_inner"] = np.concatenate([high, high, low], axis=1)
    for name, first, last in (("search", -EDGE, CYCLE - EDGE), ("around", 1 - EDGE, CYCLE - EDGE + 1)):
        real = (edge_place >= first) & (edge_place < last)
        real &= (lane < EDGE) | (lane >= LANES - EDGE)
        high, low = two_np(across(edge_place, real))
        made["edge_" + name] = np.concatenate([high, low], axis=0)
        sums.append(sums[0] + (high.astype(np.float64) + low.astype(np.float64)).sum(0))
        high, low = two_np(down(row, (row >= first) & (row < last)))
        made["down_" + name] = np.concatenate([high, high, low], axis=1)
    made["sums"] = np.concatenate([np.stack(sums), np.zeros((5, WIDE))], axis=0).astype(np.float32)
    lag = np.concatenate([np.arange(0, SHIFTS, 2), np.arange(1, SHIFTS, 2)]) - EDGE
    weight = np.where(freq == 0, 1.0, 2.0)
    phase = angle * lag[:, None] * freq[None, :]
    back = np.concatenate([np.cos(phase) * weight, np.sin(phase) * weight], axis=1)
    high, low = two_np(back)
    made["back_down"] = np.concatenate([high, high, low], axis=1)
    lag = np.arange(LANES) % SHIFTS - EDGE
    phase = angle * freq[:, None] * lag[None, :]
    back = np.zeros((WIDE, LANES))
    back[:BINS] = np.cos(phase) * weight[:, None]
    back[LANES : LANES + BINS] = np.sin(phase) * weight[:, None]
    high, low = two_np(back)
    made["back_across"] = np.concatenate([high, high, low], axis=0)
    return made


NAMES = (
    "inner",
    "edge_search",
    "edge_around",
    "down_inner",
    "down_search",
    "down_around",
    "back_down",
    "back_across",
    "sums",
)


def dot(a, b):
    return jnp.dot(a, b, preferred_element_type=F32)


def thrice(x):
    high, low = two(x)
    return jnp.concatenate([high, low, high], axis=0)


def statistics(patch):
    count = PATCH_SIDE * PATCH_SIDE
    mean = jnp.sum(patch) / count
    centered = patch - mean
    return mean, lax.rsqrt(jnp.full((1, LANES), jnp.sum(centered * centered) / count + EPSILON))


def spectra(inner, edge, mean, table, name, row):
    core = dot(jnp.concatenate([inner, inner], axis=1), table["inner"][...])
    rim = dot(jnp.concatenate([edge, edge], axis=1), table["edge_" + name][...])
    sums = table["sums"]
    full = core + rim - mean * sums[row : row + 1, :]
    core = core[EDGE : EDGE + PATCH_SIDE] - mean * sums[0:1, :]
    return dot(table["down_" + name][...], thrice(full)), dot(table["down_inner"][...], thrice(core))


def quarters(x):
    return x[:BINS, :LANES], x[BINS:, :LANES], x[:BINS, LANES:], x[BINS:, LANES:]


def matched(x, y):
    x0, x1, x2, x3 = quarters(x)
    y0, y1, y2, y3 = quarters(y)
    return (
        x0 * y0 + x1 * y1 + x2 * y2 + x3 * y3,
        x1 * y0 - x0 * y1 + x3 * y2 - x2 * y3,
        x2 * y0 - x0 * y2 + x3 * y1 - x1 * y3,
        x0 * y3 + x3 * y0 - x1 * y2 - x2 * y1,
    )


def kernel(owner, tile, offset, valid, first, second, *refs):
    table = dict(zip(NAMES, refs[: len(NAMES)]))
    out_ref, middle_ref, side_ref = refs[len(NAMES) :]
    patch_count = out_ref.shape[0]
    per_row = second.shape[2] // LANES
    tiles = second.shape[0] * per_row
    lane = lax.broadcasted_iota(jnp.int32, (1, LANES), 1)
    halves = lane < LANES // 2

    def one(k, carry):
        top = pl.multiple_of(k // per_row * PATCH_SIDE + HALO - EDGE, 16)
        rows = pl.ds(top, SEARCH)

        def place_of(c):
            return pl.ds(pl.multiple_of(c * LANES, LANES), LANES)

        here = k % per_row
        inner_a = first[rows, place_of(here + 1)]
        edge_a = jnp.where(halves, first[rows, place_of(here + 2)], first[rows, place_of(here)])
        mean_a, gain_a = statistics(inner_a[EDGE : EDGE + PATCH_SIDE].astype(F32))

        place = owner[k] * per_row + tile[k] % per_row
        row = tile[k] // per_row * PATCH_SIDE + HALO - EDGE + offset[2 * k]
        base = jnp.minimum(row // 16 * 16, second.shape[1] - ROWS)
        rows = pl.ds(pl.multiple_of(base, 16), ROWS)

        def block(c):
            c = jnp.clip(c, 0, tiles - 1)
            return second[c // per_row, rows, place_of(c % per_row)].astype(F32)

        right_end = jnp.where(place == tiles - 1, 0, LANES // 2)
        left_start = jnp.where(place == 0, LANES, LANES // 2)
        middle_ref[...] = block(place)
        side_ref[...] = jnp.where(
            lane < right_end, block(place + 1), jnp.where(lane >= left_start, block(place - 1), 0.0)
        )
        rows = pl.ds(row - base, SEARCH)
        dx = offset[2 * k + 1]
        turn = jnp.where(dx > 0, LANES - dx, -dx)
        middle = pltpu.roll(middle_ref[rows, :], turn, 1)
        side = pltpu.roll(side_ref[rows, :], turn, 1)
        within = (lane + dx >= 0) & (lane + dx < LANES)
        inner_s = jnp.where(within, middle, side)
        edge_s = jnp.where(within, side, middle).astype(BF16)
        mean_s, gain_s = statistics(inner_s[EDGE : EDGE + PATCH_SIDE])
        inner_s = inner_s.astype(BF16)

        around, around_inner = spectra(inner_a, edge_a, mean_a, table, "around", 2)
        search, search_inner = spectra(inner_s, edge_s, mean_s, table, "search", 1)
        scale = valid[k].astype(F32) / (2.0 * PATCH_SIDE * CYCLE * CYCLE)
        gain_a, gain_s = gain_a * scale, gain_s * scale
        a, b, c, d = [
            gain_a * ahead + gain_s * behind
            for ahead, behind in zip(matched(search, around_inner), matched(search_inner, around))
        ]
        spectrum = jnp.concatenate(
            [jnp.concatenate([a, c], axis=1), jnp.concatenate([b, d], axis=1)], axis=0
        )
        lines = dot(table["back_down"][...], thrice(spectrum))
        high, low = two(lines)
        surface = dot(jnp.concatenate([high, low, high], axis=1), table["back_across"][...])
        half = SHIFTS // 2
        out_ref[k] = jnp.where(halves, surface[:half], surface[half:])
        return carry

    lax.fori_loop(0, patch_count, one, 0)


def surfaces(first, gathered, owner, tile, offset, valid):
    patch_count = owner.shape[0]
    made = tables()
    return pl.pallas_call(
        kernel,
        out_shape=jax.ShapeDtypeStruct((patch_count, SHIFTS // 2, 2 * SHIFTS), F32),
        in_specs=[pl.BlockSpec(memory_space=pltpu.SMEM)] * 4
        + [pl.BlockSpec(memory_space=pltpu.VMEM)] * (2 + len(NAMES)),
        out_specs=pl.BlockSpec(memory_space=pltpu.VMEM),
        scratch_shapes=[pltpu.VMEM((ROWS, LANES), F32)] * 2,
    )(owner, tile, offset, valid, first, gathered, *[jnp.asarray(made[n]) for n in NAMES])


def both_ways(axis, tail, head):
    count = lax.axis_size(axis)
    before = lax.ppermute(tail, axis, [(i, i + 1) for i in range(count - 1)])
    after = lax.ppermute(head, axis, [(i + 1, i) for i in range(count - 1)])
    return before, after


def on_device(first_scene, second_scene, owner_strip, target_tile, offsets, valid_mask):
    per_row = first_scene.shape[1] // PATCH_SIDE
    patch_count = first_scene.shape[0] // PATCH_SIDE * per_row
    above, below = both_ways(
        "band",
        jnp.concatenate([first_scene[-HALO:], second_scene[-HALO:]], axis=0),
        jnp.concatenate([first_scene[:HALO], second_scene[:HALO]], axis=0),
    )
    second = jnp.concatenate([above[HALO:], second_scene, below[HALO:]], axis=0)
    gathered = lax.all_gather(second, "strip", axis=0)
    first = jnp.concatenate([above[:HALO], first_scene, below[:HALO]], axis=0)
    before, after = both_ways("strip", first[:, -LANES:], first[:, :LANES])
    first = jnp.concatenate([before, first, after], axis=1)
    result = surfaces(
        first,
        gathered,
        owner_strip.reshape(patch_count),
        target_tile.reshape(patch_count),
        offsets.reshape(2 * patch_count),
        valid_mask.reshape(patch_count),
    )
    return result.reshape(1, 1, patch_count, SHIFTS * SHIFTS)


def solution(mesh):
    return jax.shard_map(
        on_device,
        mesh=mesh,
        in_specs=(
            P("band", "strip"),
            P("band", "strip"),
            P("band", "strip", None, None),
            P("band", "strip", None),
            P("band", "strip", None, None),
            P("band", "strip", None),
        ),
        out_specs=P("band", "strip", None, None),
        check_vma=False,
    )
```

time: 148 us -> 96.6 us (0.65)
  Pallas kernels: 76.4 us -> 25 us
    pallas_call x1, Pallas kernels: 76.4 us -> 25 us  [surfaces(): pl.pallas_call(kernel, out_shape=jax.ShapeDtypeStruct((patch_count, SHIFT...]
  transfers between devices with their start and end apart: 5 -> 5, of which waited for: 4 -> 4; matrix products, arithmetic and copies ran while one was open for 1% -> 2% of each run, Pallas kernels for 0% -> 0%
where the time goes in v1:
time: 96.6 us; the launch traced here: 96.3 us
  waiting for transfers between devices  42.5 us (44%)
  Pallas kernels  25 us (26%)
  between operations  13.5 us (14%)
  starting transfers between devices  8.85 us (9%)
  local copies, waits for them, and re-layouts  3.43 us (4%)
  other arithmetic  3.05 us (3%)
    all_gather x1, waiting for transfers between devices, on_device(): gathered = lax.all_gather(second, 'strip', axis=0)  33.9 us
    pallas_call x1, Pallas kernels, surfaces(): pl.pallas_call(kernel, out_shape=jax.ShapeDtypeStruct((patch_count, SHIFT...  25 us
    ppermute x2, waiting for transfers between devices, both_ways(): after = lax.ppermute(head, axis, [(i + 1, i) for i in range(count - 1)])  7.14 us
    ppermute x2, starting transfers between devices, both_ways(): before = lax.ppermute(tail, axis, [(i, i + 1) for i in range(count - 1)])  6.26 us
    ppermute x2, starting transfers between devices, both_ways(): after = lax.ppermute(head, axis, [(i + 1, i) for i in range(count - 1)])  2.58 us
    concatenate x1, other arithmetic, on_device(): second = jnp.concatenate([above[HALO:], second_scene, below[HALO:]], axis=0)  1.93 us
  transfers between devices with their start and end apart: 5, of which 4 were waited for; matrix products, arithmetic and copies ran while one was open for 2% of the time, Pallas kernels for 0%

profile of v1, /device:TPU:0, one launch (start us, length us, event | category | flops | bytes accessed | tf_op | source)
XLA Modules:
  0.0 96.3 jit_solution(11558012389720638622)
XLA Ops:
  6.5 0.0 copy-start
  6.5 0.0 all-gather.3.cloned.1.call-start
  6.5 1.0 %fusion = (bf16[64,512]{1,0:T(8,128)(2,1)S(1)}, bf16[64,512]{1,0:T(8,128)(2,1)S(1)}, bf16[64,512]{1,0:T(8,128)(2,1)S(1)}, bf16[64,512]{1,0:T(8,128)(2,1)S(1)}) fusion(bf16[512,512]{1,0:T(8,128)(2,1)} %param.15, bf16[512,512]{1,0:T(8,128)(2,1)} %param.16), kind=kLoop, calls=%fused_computation.7 | loop fusion | bytes 524288 | tf_op jit(solution)/shard_map/slice | solution.py:234
  7.6 0.0 copy-start.1
  7.6 5.0 %collective-permute-start = (bf16[128,512]{1,0:T(8,128)(2,1)S(1)}, bf16[128,512]{1,0:T(8,128)(2,1)S(1)}, u32[]{:S(2)}, u32[]{:S(2)}) collective-permute-start(bf16[128,512]{1,0:T(8,128)(2,1)S(1)} %pad_maximum_fusion.5), channel_id=1, source_target_pairs={{0,8},{8,16},{16,24},{1,9},{9,17},{17,25},{2,10},{10,18},{18,26},{... | collective-permute-start | bytes 393224 | tf_op jit(solution)/shard_map/ppermute | solution.py:224
  12.6 1.3 %collective-permute-start.1 = (bf16[128,512]{1,0:T(8,128)(2,1)S(1)}, bf16[128,512]{1,0:T(8,128)(2,1)S(1)}, u32[]{:S(2)}, u32[]{:S(2)}) collective-permute-start(bf16[128,512]{1,0:T(8,128)(2,1)S(1)} %pad_maximum_fusion.6), channel_id=1, source_target_pairs={{8,0},{16,8},{24,16},{9,1},{17,9},{25,17},{10,2},{18,10},{26,18},{... | collective-permute-start | bytes 393224 | tf_op jit(solution)/shard_map/ppermute | solution.py:225
  13.9 1.4 %collective-permute-done = bf16[128,512]{1,0:T(8,128)(2,1)S(1)} collective-permute-done((bf16[128,512]{1,0:T(8,128)(2,1)S(1)}, bf16[128,512]{1,0:T(8,128)(2,1)S(1)}, u32[]{:S(2)}, u32[]{:S(2)}) %collective-permute-start) | collective-permute-done | bytes 131104 | tf_op jit(solution)/shard_map/ppermute | solution.py:224
  15.3 4.1 %collective-permute-done.1 = bf16[128,512]{1,0:T(8,128)(2,1)S(1)} collective-permute-done((bf16[128,512]{1,0:T(8,128)(2,1)S(1)}, bf16[128,512]{1,0:T(8,128)(2,1)S(1)}, u32[]{:S(2)}, u32[]{:S(2)}) %collective-permute-start.1) | collective-permute-done | bytes 131104 | tf_op jit(solution)/shard_map/ppermute | solution.py:225
  19.4 1.9 %pad_maximum_fusion.1 = bf16[640,512]{1,0:T(8,128)(2,1)} fusion(bf16[64,512]{1,0:T(8,128)(2,1)S(1)} %get-tuple-element.13, bf16[512,512]{1,0:T(8,128)(2,1)} %param.16, bf16[64,512]{1,0:T(8,128)(2,1)S(1)} %get-tuple-element.11), kind=kLoop, calls=%fused_computation.1 | loop fusion | flops 1966080 | bytes 1310720 | tf_op jit(solution)/shard_map/concatenate | solution.py:237
  21.4 0.0 all-gather.3.cloned.1.call-update
  21.4 0.0 copy-done
  21.4 1.3 %collective-permute-start.2 = (bf16[640,128]{1,0:T(8,128)(2,1)S(1)}, bf16[640,128]{1,0:T(8,128)(2,1)S(1)}, u32[]{:S(2)}, u32[]{:S(2)}) collective-permute-start(bf16[640,128]{1,0:T(8,128)(2,1)S(1)} %get-tuple-element.5), channel_id=1, source_target_pairs={{0,1},{1,2},{2,3},{3,4},{4,5},{5,6},{6,7},{8,9},{9,10},{10,11},{11... | collective-permute-start | bytes 491528 | tf_op jit(solution)/shard_map/ppermute | solution.py:224
  22.8 1.3 %collective-permute-start.3 = (bf16[640,128]{1,0:T(8,128)(2,1)S(1)}, bf16[640,128]{1,0:T(8,128)(2,1)S(1)}, u32[]{:S(2)}, u32[]{:S(2)}) collective-permute-start(bf16[640,128]{1,0:T(8,128)(2,1)S(1)} %get-tuple-element.6), channel_id=1, source_target_pairs={{1,0},{2,1},{3,2},{4,3},{5,4},{6,5},{7,6},{9,8},{10,9},{11,10},{12... | collective-permute-start | bytes 491528 | tf_op jit(solution)/shard_map/ppermute | solution.py:225
  24.1 0.0 copy-done.1
  24.1 0.1 copy.17
  24.2 0.6 reshape.17.offset
  24.8 0.0 collective-permute-done.2
  24.8 3.0 %collective-permute-done.3 = bf16[640,128]{1,0:T(8,128)(2,1)S(1)} collective-permute-done((bf16[640,128]{1,0:T(8,128)(2,1)S(1)}, bf16[640,128]{1,0:T(8,128)(2,1)S(1)}, u32[]{:S(2)}, u32[]{:S(2)}) %collective-permute-start.3) | collective-permute-done | bytes 163872 | tf_op jit(solution)/shard_map/ppermute | solution.py:225
  27.8 1.1 %pad_maximum_fusion.first = bf16[640,768]{1,0:T(8,128)(2,1)} fusion(bf16[640,128]{1,0:T(8,128)(2,1)S(1)} %collective-permute-done.3, bf16[64,512]{1,0:T(8,128)(2,1)S(1)} %get-tuple-element.14, bf16[512,512]{1,0:T(8,128)(2,1)S(1)} %copy-done, bf16[64,512]{1,0:T(8,128)(2,1)S(1)} %get-tuple-element.12, bf16[640,128]{1,0:T(8,128)(2,1)S(1)} %collective-permute-done.2), kind=kLoop, calls=%fused_computation | loop fusion | flops 4915200 | bytes 1966080 | tf_op jit(solution)/shard_map/concatenate | solution.py:241
  28.8 33.9 %all-gather.3.cloned.1.call-done = bf16[5120,512]{1,0:T(8,128)(2,1)} async-done(((bf16[640,512]{1,0:T(8,128)(2,1)}), bf16[5120,512]{1,0:T(8,128)(2,1)}) %all-gather.3.cloned.1.call-update) | async-done | bytes 5242896 | tf_op jit(solution)/shard_map/all_gather | solution.py:238
  62.8 25.0 %shard_map.145 = f32[16,32,128]{2,1,0:T(8,128)} custom-call(s32[16]{0:T(128)} %bitcast.7, s32[16]{0:T(128)} %bitcast.8, s32[32]{0:T(128)} %reshape.17.offset, s32[16]{0:T(128)} %bitcast.9, bf16[640,768]{1,0:T(8,128)(2,1)} %pad_maximum_fusion.first, bf16[8,640,512]{2,1,0:T(8,128)(2,1)} %bitcast.6, bf16[256,256]{1,0:T(8,128)(2,1)} %constant.18.clone.refs_0_, ...), custom_call_target="tpu_custom_call" | custom-call | tf_op jit(solution)/shard_map/pallas_call | solution.py:212
  87.8 1.7 %reshape.19 = f32[1,1,16,4096]{3,2,1,0:T(8,128)} reshape(f32[16,32,128]{2,1,0:T(8,128)} %shard_map.145) | data formatting | bytes 524288 | tf_op jit(solution)/shard_map/reshape | solution.py:250
  (5 shorter events, 0.1 us)
Async XLA Ops:
  6.5 14.9 %copy-start = (bf16[512,512]{1,0:T(8,128)(2,1)S(1)}, bf16[512,512]{1,0:T(8,128)(2,1)}, u32[]{:S(2)}) copy-start(bf16[512,512]{1,0:T(8,128)(2,1)} %param.15) | copy-start | bytes 1572868
  6.5 56.2 %all-gather.3.cloned.1.call-start = ((), (), s32[]{:S(2)}) async-start(), calls=%async_computation | async-start | bytes 5898240 | tf_op jit(solution)/shard_map/all_gather | solution.py:238
  7.6 16.5 %copy-start.1 = (s32[1,1,16,2]{2,3,1,0:T(2,128)S(1)}, s32[1,1,16,2]{2,3,1,0:T(2,128)}, u32[]{:S(2)}) copy-start(s32[1,1,16,2]{2,3,1,0:T(2,128)} %param.19) | copy-start | bytes 388
  7.6 7.7 %collective-permute-start = (bf16[128,512]{1,0:T(8,128)(2,1)S(1)}, bf16[128,512]{1,0:T(8,128)(2,1)S(1)}, u32[]{:S(2)}, u32[]{:S(2)}) collective-permute-start(bf16[128,512]{1,0:T(8,128)(2,1)S(1)} %pad_maximum_fusion.5), channel_id=1, source_target_pairs={{0,8},{8,16},{16,24},{1,9},{9,17},{17,25},{2,10},{10,18},{18,26},{... | collective-permute-start | bytes 393224 | tf_op jit(solution)/shard_map/ppermute | solution.py:224
  12.6 6.9 %collective-permute-start.1 = (bf16[128,512]{1,0:T(8,128)(2,1)S(1)}, bf16[128,512]{1,0:T(8,128)(2,1)S(1)}, u32[]{:S(2)}, u32[]{:S(2)}) collective-permute-start(bf16[128,512]{1,0:T(8,128)(2,1)S(1)} %pad_maximum_fusion.6), channel_id=1, source_target_pairs={{8,0},{16,8},{24,16},{9,1},{17,9},{25,17},{10,2},{18,10},{26,18},{... | collective-permute-start | bytes 393224 | tf_op jit(solution)/shard_map/ppermute | solution.py:225
  21.4 3.3 %collective-permute-start.2 = (bf16[640,128]{1,0:T(8,128)(2,1)S(1)}, bf16[640,128]{1,0:T(8,128)(2,1)S(1)}, u32[]{:S(2)}, u32[]{:S(2)}) collective-permute-start(bf16[640,128]{1,0:T(8,128)(2,1)S(1)} %get-tuple-element.5), channel_id=1, source_target_pairs={{0,1},{1,2},{2,3},{3,4},{4,5},{5,6},{6,7},{8,9},{9,10},{10,11},{11... | collective-permute-start | bytes 491528 | tf_op jit(solution)/shard_map/ppermute | solution.py:224
  22.8 5.0 %collective-permute-start.3 = (bf16[640,128]{1,0:T(8,128)(2,1)S(1)}, bf16[640,128]{1,0:T(8,128)(2,1)S(1)}, u32[]{:S(2)}, u32[]{:S(2)}) collective-permute-start(bf16[640,128]{1,0:T(8,128)(2,1)S(1)} %get-tuple-element.6), channel_id=1, source_target_pairs={{1,0},{2,1},{3,2},{4,3},{5,4},{6,5},{7,6},{9,8},{10,9},{11,10},{12... | collective-permute-start | bytes 491528 | tf_op jit(solution)/shard_map/ppermute | solution.py:225
Sparse Core Ops, SparseCore 0:
  21.5 41.2 all-gather.2

commit v2 on v1

--- a/solution.py
+++ b/solution.py
@@ -148,7 +148,7 @@
     halves = lane < LANES // 2
 
     def one(k, carry):
-        top = pl.multiple_of(k // per_row * PATCH_SIDE + HALO - EDGE, 16)
+        top = pl.multiple_of(k // per_row * PATCH_SIDE, 16)
         rows = pl.ds(top, SEARCH)
 
         def place_of(c):
@@ -219,28 +219,261 @@
     )(owner, tile, offset, valid, first, gathered, *[jnp.asarray(made[n]) for n in NAMES])
 
 
-def both_ways(axis, tail, head):
-    count = lax.axis_size(axis)
-    before = lax.ppermute(tail, axis, [(i, i + 1) for i in range(count - 1)])
-    after = lax.ppermute(head, axis, [(i + 1, i) for i in range(count - 1)])
-    return before, after
-
-
-def on_device(first_scene, second_scene, owner_strip, target_tile, offsets, valid_mask):
-    per_row = first_scene.shape[1] // PATCH_SIDE
-    patch_count = first_scene.shape[0] // PATCH_SIDE * per_row
-    above, below = both_ways(
-        "band",
-        jnp.concatenate([first_scene[-HALO:], second_scene[-HALO:]], axis=0),
-        jnp.concatenate([first_scene[:HALO], second_scene[:HALO]], axis=0),
-    )
-    second = jnp.concatenate([above[HALO:], second_scene, below[HALO:]], axis=0)
-    gathered = lax.all_gather(second, "strip", axis=0)
-    first = jnp.concatenate([above[:HALO], first_scene, below[:HALO]], axis=0)
-    before, after = both_ways("strip", first[:, -LANES:], first[:, :LANES])
-    first = jnp.concatenate([before, first, after], axis=1)
+def exchange(bands, strips, first, second, wide, gathered, zeros, *sems):
+    near_send, near_recv, side_send, side_recv, plane_send, plane_recv = sems[:6]
+    band_send, band_recv, pair_send, pair_recv, edge_send, edge_recv, local = sems[6:]
+    band, strip = lax.axis_index("band"), lax.axis_index("strip")
+    rows, cols = second.shape
+    core = strip % 2
+
+    def flip(value, bit):
+        return value + bit * (1 - 2 * (value // bit % 2))
+
+    pair = flip(strip, 1)
+    bits = [1 << i for i in range(1, strips.bit_length() - 1)]
+    turned = bits[1:] + bits[:1]
+
+    def step(value, i):
+        return flip(value, bits[i]) * (1 - core) + flip(value, turned[i]) * core
+
+    def remote(source, target, send, recv, to):
+        return pltpu.make_async_remote_copy(
+            src_ref=source,
+            dst_ref=target,
+            send_sem=send,
+            recv_sem=recv,
+            device_id=to,
+            device_id_type=pl.DeviceIdType.MESH,
+        )
+
+    has_up, has_down = band > 0, band < bands - 1
+    has_left, has_right = strip > 0, strip < strips - 1
+    up, down = (band - 1, strip), (band + 1, strip)
+    left, right = (band, strip - 1), (band, strip + 1)
+    peers = [(None, (band, pair))] + [(None, (band, step(strip, i))) for i in range(len(bits))]
+    peers += [(has_up, up), (has_down, down), (has_left, left), (has_right, right)]
+
+    barrier = pltpu.get_barrier_semaphore()
+    for there, peer in peers:
+        if there is None:
+            pl.semaphore_signal(barrier, inc=1, device_id=peer, device_id_type=pl.DeviceIdType.MESH)
+        else:
+
+            @pl.when(there)
+            def _():
+                pl.semaphore_signal(
+                    barrier, inc=1, device_id=peer, device_id_type=pl.DeviceIdType.MESH
+                )
+
+    zeros[...] = jnp.zeros_like(zeros)
+    present = [1 if there is None else there.astype(jnp.int32) for there, _ in peers]
+    pl.semaphore_wait(barrier, sum(present))
+
+    inner_rows, inner_cols = pl.ds(EDGE, rows), pl.ds(LANES, cols)
+    top_rows, bottom_rows = pl.ds(0, EDGE), pl.ds(EDGE + rows, EDGE)
+    own_first = pltpu.make_async_copy(first, wide.at[inner_rows, inner_cols], local.at[0])
+    own_second = pltpu.make_async_copy(second, gathered.at[strip, pl.ds(HALO, rows), :], local.at[1])
+    near_up = remote(
+        first.at[pl.ds(0, EDGE), :],
+        wide.at[bottom_rows, inner_cols],
+        near_send.at[0],
+        near_recv.at[0],
+        up,
+    )
+    near_down = remote(
+        first.at[pl.ds(rows - EDGE, EDGE), :],
+        wide.at[top_rows, inner_cols],
+        near_send.at[1],
+        near_recv.at[1],
+        down,
+    )
+    own_first.start()
+
+    def when(there, action):
+        if there is None:
+            action()
+        else:
+            pl.when(there)(action)
+
+    when(has_up, near_up.start)
+    when(has_down, near_down.start)
+
+    middle = (rows - 2 * HALO) // 3
+    spans = [(0, HALO), (rows - HALO, HALO)]
+    spans += [(HALO + i * middle, middle) for i in range(3)]
+    held = [strip]
+
+    def piece(block, q):
+        low, size = spans[q]
+        return gathered.at[block, pl.ds(HALO + low, size), :]
+
+    def halo(block, side):
+        return gathered.at[block, pl.ds(HALO + rows if side == 0 else 0, HALO), :]
+
+    pending = []
+
+    def along_band(j, q, source):
+        low, size = spans[q]
+        to, there = (up, has_up) if q == 0 else (down, has_down)
+        copy = remote(source, halo(held[j], q), band_send.at[j, q], band_recv.at[j, q], to)
+        when(there, copy.start)
+        pending.append((there, copy.wait_send))
+
+    def to_pair(j, q, source):
+        copy = remote(
+            source, piece(held[j], q), pair_send.at[j, q], pair_recv.at[j, q], (band, pair)
+        )
+        copy.start()
+        pending.append((None, copy.wait_send))
+        pending.append((None, copy.wait_recv))
+
+    arriving = {}
+
+    def in_plane(j, q, i, source):
+        new = j + (1 << i)
+        copy = remote(
+            source,
+            piece(held[j], q),
+            plane_send.at[new, q],
+            plane_recv.at[new, q],
+            (band, step(strip, i)),
+        )
+        copy.start()
+        pending.append((None, copy.wait_send))
+        arriving[new, q] = copy
+
+    for q, (low, size) in enumerate(spans):
+        source = second.at[pl.ds(low, size), :]
+        for i in range(len(bits)):
+            in_plane(0, q, i, source)
+        if q < 2:
+            along_band(0, q, source)
+        to_pair(0, q, source)
+    own_second.start()
+
+    top_zero = pltpu.make_async_copy(zeros.at[pl.ds(0, EDGE), :], wide.at[top_rows, inner_cols], local.at[2])
+    bottom_zero = pltpu.make_async_copy(
+        zeros.at[pl.ds(0, EDGE), :], wide.at[bottom_rows, inner_cols], local.at[3]
+    )
+    absent = [(band == 0, top_zero), (band == bands - 1, bottom_zero)]
+    left_zero = pltpu.make_async_copy(
+        zeros.at[:, pl.ds(0, LANES)], wide.at[:, pl.ds(0, LANES)], local.at[4]
+    )
+    right_zero = pltpu.make_async_copy(
+        zeros.at[:, pl.ds(0, LANES)], wide.at[:, pl.ds(LANES + cols, LANES)], local.at[5]
+    )
+    late = [(strip == 0, left_zero), (strip == strips - 1, right_zero)]
+    for block in range(strips):
+        for side in range(2):
+            fill = pltpu.make_async_copy(
+                zeros.at[pl.ds(0, HALO), :], halo(block, side), local.at[6 + 2 * block + side]
+            )
+            late.append((band == (bands - 1 if side == 0 else 0), fill))
+    for there, fill in absent + late:
+        when(there, fill.start)
+
+    own_first.wait()
+    for there, fill in absent:
+        when(there, fill.wait)
+    when(has_down, near_up.wait_recv)
+    when(has_up, near_down.wait_recv)
+    side_right = remote(
+        wide.at[:, pl.ds(cols, LANES)],
+        wide.at[:, pl.ds(0, LANES)],
+        side_send.at[0],
+        side_recv.at[0],
+        right,
+    )
+    side_left = remote(
+        wide.at[:, pl.ds(LANES, LANES)],
+        wide.at[:, pl.ds(LANES + cols, LANES)],
+        side_send.at[1],
+        side_recv.at[1],
+        left,
+    )
+    when(has_right, side_right.start)
+    when(has_left, side_left.start)
+
+    for i in range(len(bits)):
+        held += [step(value, i) for value in held]
+
+    order = []
+    for i in range(len(bits)):
+        group = [j for j in range(1, len(held)) if bin(j).count("1") == i + 1]
+        order += [(j, q) for q in range(len(spans)) for j in group]
+    for j, q in order:
+        arriving[j, q].wait_recv()
+        source = piece(held[j], q)
+        for i in range(j.bit_length(), len(bits)):
+            in_plane(j, q, i, source)
+        if q < 2:
+            along_band(j, q, source)
+        to_pair(j, q, source)
+
+    for j in range(len(held)):
+        for side, there in ((0, has_down), (1, has_up)):
+            target = halo(held[j], side)
+            seen = remote(
+                target, target, band_send.at[j, side], band_recv.at[j, side], (band, pair)
+            )
+            copy = remote(
+                target, target, edge_send.at[j, side], edge_recv.at[j, side], (band, pair)
+            )
+            when(there, seen.wait_recv)
+            when(there, copy.start)
+            pending.append((there, copy.wait_send))
+            pending.append((there, copy.wait_recv))
+
+    when(has_left, side_right.wait_recv)
+    when(has_right, side_left.wait_recv)
+    when(has_right, side_right.wait_send)
+    when(has_left, side_left.wait_send)
+    when(has_up, near_up.wait_send)
+    when(has_down, near_down.wait_send)
+    own_second.wait()
+    for there, fill in late:
+        when(there, fill.wait)
+    for there, wait in pending:
+        when(there, wait)
+
+
+def gather(bands, strips, first, second):
+    rows, cols = second.shape
+    held = max(strips // 2, 1)
+    dma = pltpu.SemaphoreType.DMA
+    return pl.pallas_call(
+        functools.partial(exchange, bands, strips),
+        out_shape=(
+            jax.ShapeDtypeStruct((rows + 2 * EDGE, cols + 2 * LANES), first.dtype),
+            jax.ShapeDtypeStruct((strips, rows + 2 * HALO, cols), second.dtype),
+        ),
+        in_specs=[pl.BlockSpec(memory_space=pltpu.VMEM)] * 2,
+        out_specs=[pl.BlockSpec(memory_space=pl.ANY)] * 2,
+        scratch_shapes=[
+            pltpu.VMEM((rows + 2 * EDGE, cols), second.dtype),
+            dma((2,)),
+            dma((2,)),
+            dma((2,)),
+            dma((2,)),
+            dma((held, 5)),
+            dma((held, 5)),
+            dma((held, 2)),
+            dma((held, 2)),
+            dma((held, 5)),
+            dma((held, 5)),
+            dma((held, 2)),
+            dma((held, 2)),
+            dma((6 + 2 * strips,)),
+        ],
+        compiler_params=pltpu.CompilerParams(collective_id=0, has_side_effects=True),
+    )(first, second)
+
+
+def on_device(bands, strips, first_scene, second_scene, owner_strip, target_tile, offsets, valid_mask):
+    patch_count = target_tile.shape[-1]
+    wide, gathered = gather(bands, strips, first_scene, second_scene)
     result = surfaces(
-        first,
+        wide,
         gathered,
         owner_strip.reshape(patch_count),
         target_tile.reshape(patch_count),
@@ -252,7 +485,7 @@
 
 def solution(mesh):
     return jax.shard_map(
-        on_device,
+        functools.partial(on_device, mesh.shape["band"], mesh.shape["strip"]),
         mesh=mesh,
         in_specs=(
             P("band", "strip"),

time: 96.6 us -> 57.6 us (0.60)
  waiting for transfers between devices: 42.5 us -> 0 us
  Pallas kernels: 25 us -> 54.4 us
  between operations: 13.5 us -> 0.01 us
  starting transfers between devices: 8.85 us -> 0 us
  other arithmetic: 3.05 us -> 0 us
    all_gather x1 -> x0, waiting for transfers between devices: 33.9 us -> none  [on_device(): gathered = lax.all_gather(second, 'strip', axis=0)]
    pallas_call x0 -> x1, Pallas kernels: none -> 29.4 us  [gather(): pl.pallas_call(functools.partial(exchange, bands, strips), out_shape=(jax...]
    ppermute x4 -> x0, starting transfers between devices: 8.85 us -> none  [the longest x2 6.26 us: both_ways(): before = lax.ppermute(tail, axis, [(i, i + 1) for i in range(count - 1)])]
    ppermute x4 -> x0, waiting for transfers between devices: 8.56 us -> none  [the longest x2 7.14 us: both_ways(): after = lax.ppermute(head, axis, [(i + 1, i) for i in range(count - 1)])]
    concatenate x4 -> x0, other arithmetic: 3.03 us -> none  [the longest x1 1.93 us: on_device(): second = jnp.concatenate([above[HALO:], second_scene, below[HALO:]], axis=0)]
    slice x3 -> x0, local copies, waits for them, and re-layouts: 1.03 us -> none  [the longest x1 1.01 us: on_device(): first_scene[-HALO:]]
  transfers between devices with their start and end apart: 5 -> 0, of which waited for: 4 -> 0; matrix products, arithmetic and copies ran while one was open for 2% -> 0% of each run, Pallas kernels for 0% -> 0%
where the time goes in v2:
time: 57.6 us; the launch traced here: 57.4 us
  Pallas kernels  54.4 us (94%)
  local copies, waits for them, and re-layouts  3.06 us (5%)
    pallas_call x1, Pallas kernels, gather(): pl.pallas_call(functools.partial(exchange, bands, strips), out_shape=(jax...  29.4 us
    pallas_call x1, Pallas kernels, surfaces(): pl.pallas_call(kernel, out_shape=jax.ShapeDtypeStruct((patch_count, SHIFT...  25 us
    reshape x1, local copies, waits for them, and re-layouts, on_device(): return result.reshape(1, 1, patch_count, SHIFTS * SHIFTS)  1.7 us

profile of v2, /device:TPU:0, one launch (start us, length us, event | category | flops | bytes accessed | tf_op | source)
XLA Modules:
  0.0 57.4 jit_solution(7584628029177637988)
XLA Ops:
  0.0 0.8 %copy.17 = s32[1,1,16,2]{3,2,1,0:T(8,128)S(1)} copy(s32[1,1,16,2]{2,3,1,0:T(2,128)} %param.19) | data formatting | bytes 256 | tf_op args[4]
  0.8 0.6 %reshape.17.offset = s32[32]{0:T(128)} reshape(s32[1,1,16,2]{3,2,1,0:T(8,128)S(1)} %copy.17) | data formatting | bytes 256 | tf_op jit(solution)/shard_map/reshape | solution.py:480
  1.4 29.4 %shard_map.145 = (bf16[576,768]{1,0:T(8,128)(2,1)}, bf16[8,640,512]{2,1,0:T(8,128)(2,1)}) custom-call(bf16[512,512]{1,0:T(8,128)(2,1)} %first.1, bf16[512,512]{1,0:T(8,128)(2,1)} %second.1), custom_call_target="tpu_custom_call" | custom-call | tf_op jit(solution)/shard_map/pallas_call | solution.py:444
  30.8 25.0 %shard_map.146 = f32[16,32,128]{2,1,0:T(8,128)} custom-call(s32[16]{0:T(128)} %bitcast.5, s32[16]{0:T(128)} %bitcast.6, s32[32]{0:T(128)} %reshape.17.offset, s32[16]{0:T(128)} %bitcast.7, bf16[576,768]{1,0:T(8,128)(2,1)} %get-tuple-element.7.first, bf16[8,640,512]{2,1,0:T(8,128)(2,1)} %get-tuple-element.8.second, bf16[256,256]{1,0:T(8,128)(2,1)} %constant.18.clone.refs_0_, ...), custom_call_target="tpu_custom_call" | custom-call | tf_op jit(solution)/shard_map/pallas_call | solution.py:212
  55.7 1.7 %reshape.19 = f32[1,1,16,4096]{3,2,1,0:T(8,128)} reshape(f32[16,32,128]{2,1,0:T(8,128)} %shard_map.146) | data formatting | bytes 524288 | tf_op jit(solution)/shard_map/reshape | solution.py:483

commit v3 on v1

v3 whole, which is shorter than its diff:
```python
import functools

import jax
import jax.numpy as jnp
import numpy as np
from jax import lax
from jax.experimental import pallas as pl
from jax.experimental.pallas import tpu as pltpu
from jax.sharding import PartitionSpec as P

PATCH_SIDE = 128
SHIFTS = 64
EDGE = SHIFTS // 2
SEARCH = PATCH_SIDE + SHIFTS
CYCLE = SEARCH - 1
BINS = (CYCLE + 1) // 2
LANES = 128
WIDE = 2 * LANES
HALO = 64
ROWS = SEARCH + 16
SPLIT = 3
GROUPS = 4
EACH = 2
EPSILON = 1e-05
F32 = jnp.float32
BF16 = jnp.bfloat16


def two(x):
    high = x.astype(BF16)
    return high, (x - high.astype(F32)).astype(BF16)


def two_np(x):
    high = x.astype(jnp.bfloat16)
    low = (x - high.astype(np.float64)).astype(jnp.bfloat16)
    return high, low


def tables():
    angle = 2 * np.pi / CYCLE
    freq = np.arange(BINS)

    def across(place, real):
        out = np.zeros((LANES, WIDE))
        phase = angle * place[:, None] * freq[None, :]
        out[:, :BINS] = np.cos(phase) * real[:, None]
        out[:, LANES : LANES + BINS] = np.sin(phase) * real[:, None]
        return out

    def down(place, real):
        phase = angle * place[None, :] * freq[:, None]
        return np.concatenate([np.cos(phase), np.sin(phase)], axis=0) * real[None, :]

    lane = np.arange(LANES)
    edge_place = np.where(lane < LANES // 2, PATCH_SIDE + lane, lane - LANES)
    row = np.arange(SEARCH) - EDGE
    made = {}
    sums = []
    inner = across(lane, np.ones(LANES))
    high, low = two_np(inner)
    made["inner"] = np.concatenate([high, low], axis=0)
    sums.append((high.astype(np.float64) + low.astype(np.float64)).sum(0))
    high, low = two_np(down(row[EDGE : EDGE + PATCH_SIDE], np.ones(PATCH_SIDE)))
    made["down_inner"] = np.concatenate([high, high, low], axis=1)
    for name, first, last in (("search", -EDGE, CYCLE - EDGE), ("around", 1 - EDGE, CYCLE - EDGE + 1)):
        real = (edge_place >= first) & (edge_place < last)
        real &= (lane < EDGE) | (lane >= LANES - EDGE)
        high, low = two_np(across(edge_place, real))
        made["edge_" + name] = np.concatenate([high, low], axis=0)
        sums.append(sums[0] + (high.astype(np.float64) + low.astype(np.float64)).sum(0))
        high, low = two_np(down(row, (row >= first) & (row < last)))
        made["down_" + name] = np.concatenate([high, high, low], axis=1)
    made["sums"] = np.concatenate([np.stack(sums), np.zeros((5, WIDE))], axis=0).astype(np.float32)
    lag = np.concatenate([np.arange(0, SHIFTS, 2), np.arange(1, SHIFTS, 2)]) - EDGE
    weight = np.where(freq == 0, 1.0, 2.0)
    phase = angle * lag[:, None] * freq[None, :]
    back = np.concatenate([np.cos(phase) * weight, np.sin(phase) * weight], axis=1)
    high, low = two_np(back)
    made["back_down"] = np.concatenate([high, high, low], axis=1)
    lag = np.arange(LANES) % SHIFTS - EDGE
    phase = angle * freq[:, None] * lag[None, :]
    back = np.zeros((WIDE, LANES))
    back[:BINS] = np.cos(phase) * weight[:, None]
    back[LANES : LANES + BINS] = np.sin(phase) * weight[:, None]
    high, low = two_np(back)
    made["back_across"] = np.concatenate([high, high, low], axis=0)
    return made


FORMER = ("inner", "edge_around", "down_inner", "down_around", "sums")
LATTER = (
    "inner",
    "edge_search",
    "down_inner",
    "down_search",
    "back_down",
    "back_across",
    "sums",
)


def dot(a, b):
    return jnp.dot(a, b, preferred_element_type=F32)


def thrice(x):
    high, low = two(x)
    return jnp.concatenate([high, low, high], axis=0)


def statistics(patch):
    count = PATCH_SIDE * PATCH_SIDE
    mean = jnp.sum(patch) / count
    centered = patch - mean
    return mean, lax.rsqrt(jnp.full((1, LANES), jnp.sum(centered * centered) / count + EPSILON))


def spectra(inner, edge, mean, table, name, row):
    core = dot(jnp.concatenate([inner, inner], axis=1), table["inner"][...])
    rim = dot(jnp.concatenate([edge, edge], axis=1), table["edge_" + name][...])
    sums = table["sums"]
    full = core + rim - mean * sums[row : row + 1, :]
    core = core[EDGE : EDGE + PATCH_SIDE] - mean * sums[0:1, :]
    return dot(table["down_" + name][...], thrice(full)), dot(table["down_inner"][...], thrice(core))


def quarters(x):
    return x[:BINS, :LANES], x[BINS:, :LANES], x[:BINS, LANES:], x[BINS:, LANES:]


def matched(x, y):
    x0, x1, x2, x3 = quarters(x)
    y0, y1, y2, y3 = quarters(y)
    return (
        x0 * y0 + x1 * y1 + x2 * y2 + x3 * y3,
        x1 * y0 - x0 * y1 + x3 * y2 - x2 * y3,
        x2 * y0 - x0 * y2 + x3 * y1 - x1 * y3,
        x0 * y3 + x3 * y0 - x1 * y2 - x2 * y1,
    )


def flip(value, bit):
    return value + bit * (1 - 2 * (value // bit % 2))


def remote(source, target, send, recv, to):
    return pltpu.make_async_remote_copy(
        src_ref=source,
        dst_ref=target,
        send_sem=send,
        recv_sem=recv,
        device_id=to,
        device_id_type=pl.DeviceIdType.MESH,
    )


def when(there, action):
    if there is None:
        action()
    else:
        pl.when(there)(action)


def exchange(bands, strips, first, second, *refs):
    refs = list(refs)

    def take(count):
        taken, refs[:count] = refs[:count], []
        return taken

    stored = take(len(FORMER))
    gathered, around_out, core_out = take(3)
    wide, around_ref, core_ref, zeros = take(4)
    table_refs = take(len(FORMER))
    near_send, near_recv, plane_send, plane_recv, band_send, band_recv = take(6)
    pair_send, pair_recv, edge_send, edge_recv, local, table_sem, out_sem, fill_sem = take(8)
    table = dict(zip(FORMER, table_refs))

    band, strip = lax.axis_index("band"), lax.axis_index("strip")
    rows, cols = second.shape
    patch_count = around_ref.shape[0]
    per_row = cols // LANES
    core = strip % 2
    pair = flip(strip, 1)
    bits = [1 << i for i in range(1, strips.bit_length() - 1)]
    turned = bits[1:] + bits[:1]

    def step(value, i):
        return flip(value, bits[i]) * (1 - core) + flip(value, turned[i]) * core

    has_up, has_down = band > 0, band < bands - 1
    has_left, has_right = strip > 0, strip < strips - 1
    near = []
    for dr in (-1, 0, 1):
        for dc in (-1, 0, 1):
            if dr == 0 and dc == 0:
                continue
            there = None
            for wanted in ([has_up] if dr < 0 else [has_down] if dr > 0 else []) + (
                [has_left] if dc < 0 else [has_right] if dc > 0 else []
            ):
                there = wanted if there is None else there & wanted
            near.append((dr, dc, there))
    peers = [(None, (band, pair))] + [(None, (band, step(strip, i))) for i in range(len(bits))]
    peers += [(there, (band + dr, strip + dc)) for dr, dc, there in near]

    barrier = pltpu.get_barrier_semaphore()
    for there, peer in peers:

        def signal(peer=peer):
            pl.semaphore_signal(barrier, inc=1, device_id=peer, device_id_type=pl.DeviceIdType.MESH)

        when(there, signal)

    locals_ = [
        pltpu.make_async_copy(
            first, wide.at[pl.ds(EDGE, rows), pl.ds(LANES, cols)], local.at[0]
        ),
        pltpu.make_async_copy(second, gathered.at[strip, pl.ds(HALO, rows), :], local.at[1]),
    ]
    locals_ += [
        pltpu.make_async_copy(source, target, table_sem.at[i])
        for i, (source, target) in enumerate(zip(stored, table_refs))
    ]
    for copy in locals_:
        copy.start()

    def row_blank(low):
        wide[pl.ds(low, EDGE), :] = jnp.zeros((EDGE, cols + 2 * LANES), wide.dtype)

    def col_blank(low):
        wide[pl.ds(EDGE, rows), pl.ds(low, LANES)] = jnp.zeros((rows, LANES), wide.dtype)

    def corner_blank(there, low, left):
        @pl.when(there)
        def _():
            wide[pl.ds(low, EDGE), pl.ds(left, LANES)] = jnp.zeros((EDGE, LANES), wide.dtype)

    def halo(block, side):
        return gathered.at[block, pl.ds(HALO + rows if side == 0 else 0, HALO), :]

    zeros[...] = jnp.zeros_like(zeros)
    when(band == 0, lambda: row_blank(0))
    when(band == bands - 1, lambda: row_blank(EDGE + rows))
    when(strip == 0, lambda: col_blank(0))
    when(strip == strips - 1, lambda: col_blank(LANES + cols))
    corner_blank((strip == 0) & has_up, 0, 0)
    corner_blank((strip == 0) & has_down, EDGE + rows, 0)
    corner_blank((strip == strips - 1) & has_up, 0, LANES + cols)
    corner_blank((strip == strips - 1) & has_down, EDGE + rows, LANES + cols)

    present = [1 if there is None else there.astype(jnp.int32) for there, _ in peers]
    pl.semaphore_wait(barrier, sum(present))

    pending = []

    def part(delta, low, full, margin):
        if delta < 0:
            return pl.ds(low, margin)
        if delta > 0:
            return pl.ds(low + full - margin, margin)
        return pl.ds(low, full)

    def beyond(delta, full, margin):
        if delta < 0:
            return pl.ds(margin + full, margin)
        if delta > 0:
            return pl.ds(0, margin)
        return pl.ds(margin, full)

    nearby = []
    for i, (dr, dc, there) in enumerate(near):
        copy = remote(
            first.at[part(dr, 0, rows, EDGE), part(dc, 0, cols, LANES)],
            wide.at[beyond(dr, rows, EDGE), beyond(dc, cols, LANES)],
            near_send.at[i],
            near_recv.at[i],
            (band + dr, strip + dc),
        )
        when(there, copy.start)
        pending.append((there, copy.wait_send))
        back = [t for r, c, t in near if r == -dr and c == -dc][0]
        nearby.append((back, copy.wait_recv))

    middle = (rows - 2 * HALO) // SPLIT
    spans = [(0, HALO), (rows - HALO, HALO)]
    spans += [(HALO + i * middle, middle) for i in range(SPLIT)]
    held = [strip]

    def piece(block, q):
        low, size = spans[q]
        return gathered.at[block, pl.ds(HALO + low, size), :]

    def along_band(j, q, source):
        to, there = (up, has_up) if q == 0 else (down, has_down)
        copy = remote(source, halo(held[j], q), band_send.at[j, q], band_recv.at[j, q], to)
        when(there, copy.start)
        pending.append((there, copy.wait_send))

    up, down = (band - 1, strip), (band + 1, strip)
    to_mate = (band, pair)

    def to_pair(j, q, source):
        copy = remote(source, piece(held[j], q), pair_send.at[j, q], pair_recv.at[j, q], to_mate)
        copy.start()
        pending.append((None, copy.wait_send))
        pending.append((None, copy.wait_recv))

    arriving = {}

    def in_plane(j, q, i, source):
        new = j + (1 << i)
        copy = remote(
            source,
            piece(held[j], q),
            plane_send.at[new, q],
            plane_recv.at[new, q],
            (band, step(strip, i)),
        )
        copy.start()
        pending.append((None, copy.wait_send))
        arriving[new, q] = copy

    for q, (low, size) in enumerate(spans):
        source = second.at[pl.ds(low, size), :]
        for i in range(len(bits)):
            in_plane(0, q, i, source)
        if q < 2:
            along_band(0, q, source)
        to_pair(0, q, source)

    for i in range(len(bits)):
        held += [step(value, i) for value in held]

    order = []
    for i in range(len(bits)):
        group = [j for j in range(1, len(held)) if bin(j).count("1") == i + 1]
        order += [(j, q) for q in range(len(spans)) for j in group]

    def forward(j, q):
        arriving[j, q].wait_recv()
        source = piece(held[j], q)
        for i in range(j.bit_length(), len(bits)):
            in_plane(j, q, i, source)
        if q < 2:
            along_band(j, q, source)
        to_pair(j, q, source)

    for block in range(strips):
        for side in range(2):
            fill = pltpu.make_async_copy(zeros, halo(block, side), fill_sem.at[block, side])
            absent = band == (bands - 1 if side == 0 else 0)
            when(absent, fill.start)
            pending.append((absent, fill.wait))
    for there, wait in nearby:
        when(there, wait)
    locals_[0].wait()
    for copy in locals_[2:]:
        copy.wait()
    pending.append((None, locals_[1].wait))

    lane = lax.broadcasted_iota(jnp.int32, (1, LANES), 1)
    halves = lane < LANES // 2

    def place_of(c):
        return pl.ds(pl.multiple_of(c * LANES, LANES), LANES)

    def results(k):
        return [
            pltpu.make_async_copy(source.at[k], target.at[k], out_sem.at[i, k])
            for i, (source, target) in enumerate(((around_ref, around_out), (core_ref, core_out)))
        ]

    def around_one(k, carry):
        top = pl.multiple_of(k // per_row * PATCH_SIDE, 16)
        window = pl.ds(top, SEARCH)
        here = k % per_row
        inner = wide[window, place_of(here + 1)]
        edge = jnp.where(halves, wide[window, place_of(here + 2)], wide[window, place_of(here)])
        mean, gain = statistics(inner[EDGE : EDGE + PATCH_SIDE].astype(F32))
        full, inside = spectra(inner, edge, mean, table, "around", 2)
        around_ref[k] = full
        core_ref[k] = inside * gain[:, :1]
        for copy in results(k):
            copy.start()
        return carry

    done = 0
    steps = len(order)
    groups = GROUPS
    for g in range(groups):
        lax.fori_loop(g * patch_count // groups, (g + 1) * patch_count // groups, around_one, 0)
        upto = (g + 1) * steps // groups
        for j, q in order[done:upto]:
            forward(j, q)
        done = upto

    for j in range(len(held)):
        for side, there in ((0, has_down), (1, has_up)):
            target = halo(held[j], side)
            seen = remote(target, target, band_send.at[j, side], band_recv.at[j, side], to_mate)
            copy = remote(target, target, edge_send.at[j, side], edge_recv.at[j, side], to_mate)
            when(there, seen.wait_recv)
            when(there, copy.start)
            pending.append((there, copy.wait_send))
            pending.append((there, copy.wait_recv))
    for there, wait in pending:
        when(there, wait)

    for k in range(patch_count):
        for copy in results(k):
            copy.wait()


def correlate(rows_total, owner, tile, offset, valid, gathered, around_ref, core_ref, *refs):
    table = dict(zip(LATTER, refs[: len(LATTER)]))
    out_ref, blocks, middle_ref, side_ref, surface_ref, sems = refs[len(LATTER) :]
    turn_id = pl.program_id(0)
    patch_count = out_ref.shape[0]
    each = around_ref.shape[0]
    per_row = gathered.shape[2] // LANES
    tiles = gathered.shape[0] * per_row
    lane = lax.broadcasted_iota(jnp.int32, (1, LANES), 1)
    halves = lane < LANES // 2
    half = SHIFTS // 2

    def place_of(k):
        place = owner[k] * per_row + tile[k] % per_row
        row = tile[k] // per_row * PATCH_SIDE + HALO - EDGE + offset[0, k]
        return place, row, jnp.minimum(row // 16 * 16, rows_total - ROWS)

    def fetch(turn, slot):
        made = []
        for n in range(each):
            place, _, base = place_of(turn * each + n)
            for c in range(3):
                block = jnp.minimum(jnp.maximum(place + c - 1, 0), tiles - 1)
                made.append(
                    pltpu.make_async_copy(
                        gathered.at[
                            block // per_row,
                            pl.ds(pl.multiple_of(base, 16), ROWS),
                            pl.ds(pl.multiple_of(block % per_row * LANES, LANES), LANES),
                        ],
                        blocks.at[slot, n, c],
                        sems.at[slot, n, c],
                    )
                )
        return made

    slot = turn_id % 2

    @pl.when(turn_id == 0)
    def _():
        for copy in fetch(0, 0):
            copy.start()

    @pl.when(turn_id + 1 < pl.num_programs(0))
    def _():
        for copy in fetch(turn_id + 1, 1 - slot):
            copy.start()

    for copy in fetch(turn_id, slot):
        copy.wait()

    for n in range(each):
        k = turn_id * each + n
        place, row, base = place_of(k)
        right_end = jnp.where(place == tiles - 1, 0, LANES // 2)
        left_start = jnp.where(place == 0, LANES, LANES // 2)
        middle_ref[n] = blocks[slot, n, 1].astype(F32)
        side_ref[n] = jnp.where(
            lane < right_end,
            blocks[slot, n, 2].astype(F32),
            jnp.where(lane >= left_start, blocks[slot, n, 0].astype(F32), 0.0),
        )
        shown = pl.ds(row - base, SEARCH)
        dx = offset[1, k]
        turn = jnp.where(dx > 0, LANES - dx, -dx)
        centre = pltpu.roll(middle_ref[n, shown, :], turn, 1)
        side = pltpu.roll(side_ref[n, shown, :], turn, 1)
        within = (lane + dx >= 0) & (lane + dx < LANES)
        inner = jnp.where(within, centre, side)
        edge = jnp.where(within, side, centre).astype(BF16)
        mean, gain = statistics(inner[EDGE : EDGE + PATCH_SIDE])
        full, inside = spectra(inner.astype(BF16), edge, mean, table, "search", 1)
        inside = inside * gain[:, :1]
        a, b, c, d = [
            ahead + behind
            for ahead, behind in zip(matched(full, core_ref[n]), matched(inside, around_ref[n]))
        ]
        spectrum = jnp.concatenate(
            [jnp.concatenate([a, c], axis=1), jnp.concatenate([b, d], axis=1)], axis=0
        )
        lines = dot(table["back_down"][...], thrice(spectrum))
        high, low = two(lines)
        surface = dot(jnp.concatenate([high, low, high], axis=1), table["back_across"][...])
        scale = valid[k].astype(F32) / (2.0 * PATCH_SIDE * CYCLE * CYCLE)
        surface_ref[pl.ds(pl.multiple_of(k * half, half), half), :] = (
            jnp.where(halves, surface[:half], surface[half:]) * scale
        )

    @pl.when(turn_id == pl.num_programs(0) - 1)
    def _():
        for r in range(half):
            out_ref[:, r * LANES : (r + 1) * LANES] = surface_ref[
                pl.ds(r, patch_count, stride=half), :
            ]


def on_device(bands, strips, first_scene, second_scene, owner_strip, target_tile, offsets, valid_mask):
    patch_count = target_tile.shape[-1]
    rows, cols = second_scene.shape
    made = tables()
    former = [jnp.asarray(made[name]) for name in FORMER]
    latter = [jnp.asarray(made[name]) for name in LATTER]
    held = max(strips // 2, 1)
    dma = pltpu.SemaphoreType.DMA
    pieces = SPLIT + 2
    spectrum = (patch_count, 2 * BINS, WIDE)
    gathered, around, core = pl.pallas_call(
        functools.partial(exchange, bands, strips),
        out_shape=(
            jax.ShapeDtypeStruct((strips, rows + 2 * HALO, cols), second_scene.dtype),
            jax.ShapeDtypeStruct(spectrum, F32),
            jax.ShapeDtypeStruct(spectrum, F32),
        ),
        in_specs=[pl.BlockSpec(memory_space=pl.ANY)] * (2 + len(FORMER)),
        out_specs=[pl.BlockSpec(memory_space=pl.ANY)] * 3,
        scratch_shapes=[
            pltpu.VMEM((rows + 2 * EDGE, cols + 2 * LANES), first_scene.dtype),
            pltpu.VMEM(spectrum, F32),
            pltpu.VMEM(spectrum, F32),
            pltpu.VMEM((HALO, cols), second_scene.dtype),
            *[pltpu.VMEM(c.shape, c.dtype) for c in former],
            dma((8,)),
            dma((8,)),
            dma((held, pieces)),
            dma((held, pieces)),
            dma((held, 2)),
            dma((held, 2)),
            dma((held, pieces)),
            dma((held, pieces)),
            dma((held, 2)),
            dma((held, 2)),
            dma((2,)),
            dma((len(FORMER),)),
            dma((2, patch_count)),
            dma((strips, 2)),
        ],
        compiler_params=pltpu.CompilerParams(collective_id=0, has_side_effects=True),
    )(first_scene, second_scene, *former)
    each = EACH
    block = pl.BlockSpec((each,) + spectrum[1:], lambda k, *_: (k, 0, 0))
    result = pl.pallas_call(
        functools.partial(correlate, rows + 2 * HALO),
        out_shape=jax.ShapeDtypeStruct((patch_count, SHIFTS * SHIFTS), F32),
        grid_spec=pltpu.PrefetchScalarGridSpec(
            num_scalar_prefetch=4,
            grid=(patch_count // each,),
            in_specs=[pl.BlockSpec(memory_space=pl.ANY), block, block]
            + [pl.BlockSpec(c.shape, lambda k, *_: (0, 0)) for c in latter],
            out_specs=pl.BlockSpec((patch_count, SHIFTS * SHIFTS), lambda k, *_: (0, 0)),
            scratch_shapes=[
                pltpu.VMEM((2, each, 3, ROWS, LANES), second_scene.dtype),
                pltpu.VMEM((each, ROWS, LANES), F32),
                pltpu.VMEM((each, ROWS, LANES), F32),
                pltpu.VMEM((patch_count * SHIFTS // 2, LANES), F32),
                dma((2, each, 3)),
            ],
        ),
    )(
        owner_strip.reshape(patch_count),
        target_tile.reshape(patch_count),
        offsets.reshape(patch_count, 2).T,
        valid_mask.reshape(patch_count),
        gathered,
        around,
        core,
        *latter,
    )
    return result.reshape(1, 1, patch_count, SHIFTS * SHIFTS)


def solution(mesh):
    return jax.shard_map(
        functools.partial(on_device, mesh.shape["band"], mesh.shape["strip"]),
        mesh=mesh,
        in_specs=(
            P("band", "strip"),
            P("band", "strip"),
            P("band", "strip", None, None),
            P("band", "strip", None),
            P("band", "strip", None, None),
            P("band", "strip", None),
        ),
        out_specs=P("band", "strip", None, None),
        check_vma=False,
    )
```

time: 96.6 us -> 48.8 us (0.51)
  waiting for transfers between devices: 42.5 us -> 0 us
  Pallas kernels: 25 us -> 48.6 us
  between operations: 13.5 us -> 0.01 us
  starting transfers between devices: 8.85 us -> 0 us
  local copies, waits for them, and re-layouts: 3.43 us -> 0 us
  other arithmetic: 3.05 us -> 0 us
    all_gather x1 -> x0, waiting for transfers between devices: 33.9 us -> none  [on_device(): gathered = lax.all_gather(second, 'strip', axis=0)]
    pallas_call x1 -> x2, Pallas kernels: 25 us -> 48.6 us  [the longest x1 29.3 us: on_device(): pl.pallas_call(functools.partial(exchange, bands, strips), out_shape=(jax...]
    ppermute x4 -> x0, starting transfers between devices: 8.85 us -> none  [the longest x2 6.26 us: both_ways(): before = lax.ppermute(tail, axis, [(i, i + 1) for i in range(count - 1)])]
    ppermute x4 -> x0, waiting for transfers between devices: 8.56 us -> none  [the longest x2 7.14 us: both_ways(): after = lax.ppermute(head, axis, [(i + 1, i) for i in range(count - 1)])]
    concatenate x4 -> x0, other arithmetic: 3.03 us -> none  [the longest x1 1.93 us: on_device(): second = jnp.concatenate([above[HALO:], second_scene, below[HALO:]], axis=0)]
    reshape x2 -> x0, local copies, waits for them, and re-layouts: 2.31 us -> none  [the longest x1 1.7 us: on_device(): return result.reshape(1, 1, patch_count, SHIFTS * SHIFTS)]
    slice x3 -> x0, local copies, waits for them, and re-layouts: 1.03 us -> none  [the longest x1 1.01 us: on_device(): first_scene[-HALO:]]
  transfers between devices with their start and end apart: 5 -> 0, of which waited for: 4 -> 0; matrix products, arithmetic and copies ran while one was open for 2% -> 0% of each run, Pallas kernels for 0% -> 0%
where the time goes in v3:
time: 48.8 us; the launch traced here: 48.6 us
  Pallas kernels  48.6 us (100%)
    pallas_call x1, Pallas kernels, on_device(): pl.pallas_call(functools.partial(exchange, bands, strips), out_shape=(jax...  29.3 us
    pallas_call x1, Pallas kernels, on_device(): pl.pallas_call(functools.partial(correlate, rows + 2 * HALO), out_shape=j...  19.3 us

profile of v3, /device:TPU:0, one launch (start us, length us, event | category | flops | bytes accessed | tf_op | source)
XLA Modules:
  0.0 48.6 jit_solution(14500672277686831739)
XLA Ops:
  0.0 29.3 %shard_map.145 = (bf16[8,640,512]{2,1,0:T(8,128)(2,1)}, f32[16,192,256]{2,1,0:T(8,128)}, f32[16,192,256]{2,1,0:T(8,128)}) custom-call(bf16[512,512]{1,0:T(8,128)(2,1)} %first.1, bf16[512,512]{1,0:T(8,128)(2,1)} %second.1, bf16[256,256]{1,0:T(8,128)(2,1)} %constant.18.clone.refs_0_, bf16[256,256]{1,0:T(8,128)(2,1)} %constant.19.clone.refs_1_, ...), custom_call_target="tpu_custom_call" | custom-call | tf_op jit(solution)/shard_map/pallas_call | solution.py:522
  29.3 19.3 %shard_map.146 = f32[16,4096]{1,0:T(8,128)} custom-call(s32[16]{0:T(128)} %bitcast.8, s32[16]{0:T(128)} %bitcast.9, s32[2,16]{1,0:T(2,128)} %bitcast.7, s32[16]{0:T(128)} %bitcast.10, bf16[8,640,512]{2,1,0:T(8,128)(2,1)} %get-tuple-element.8.gathered, f32[16,192,256]{2,1,0:T(8,128)} %get-tuple-element.9.around_ref, ...), custom_call_target="tpu_custom_call" | custom-call | tf_op jit(solution)/shard_map/pallas_call | solution.py:556

commit v4 on v3

--- a/solution.py
+++ b/solution.py
@@ -19,8 +19,7 @@
 HALO = 64
 ROWS = SEARCH + 16
 SPLIT = 3
-GROUPS = 4
-EACH = 2
+EACH = 4
 EPSILON = 1e-05
 F32 = jnp.float32
 BF16 = jnp.bfloat16
@@ -62,7 +61,9 @@
     made["inner"] = np.concatenate([high, low], axis=0)
     sums.append((high.astype(np.float64) + low.astype(np.float64)).sum(0))
     high, low = two_np(down(row[EDGE : EDGE + PATCH_SIDE], np.ones(PATCH_SIDE)))
-    made["down_inner"] = np.concatenate([high, high, low], axis=1)
+    made["down_inner"] = np.concatenate(
+        [np.concatenate([high, high], axis=1), np.concatenate([low, low], axis=1)], axis=0
+    )
     for name, first, last in (("search", -EDGE, CYCLE - EDGE), ("around", 1 - EDGE, CYCLE - EDGE + 1)):
         real = (edge_place >= first) & (edge_place < last)
         real &= (lane < EDGE) | (lane >= LANES - EDGE)
@@ -70,14 +71,14 @@
         made["edge_" + name] = np.concatenate([high, low], axis=0)
         sums.append(sums[0] + (high.astype(np.float64) + low.astype(np.float64)).sum(0))
         high, low = two_np(down(row, (row >= first) & (row < last)))
-        made["down_" + name] = np.concatenate([high, high, low], axis=1)
+        made["down_" + name] = np.concatenate([high, low], axis=0)
     made["sums"] = np.concatenate([np.stack(sums), np.zeros((5, WIDE))], axis=0).astype(np.float32)
     lag = np.concatenate([np.arange(0, SHIFTS, 2), np.arange(1, SHIFTS, 2)]) - EDGE
     weight = np.where(freq == 0, 1.0, 2.0)
     phase = angle * lag[:, None] * freq[None, :]
     back = np.concatenate([np.cos(phase) * weight, np.sin(phase) * weight], axis=1)
     high, low = two_np(back)
-    made["back_down"] = np.concatenate([high, high, low], axis=1)
+    made["back_down"] = np.concatenate([high, low], axis=0)
     lag = np.arange(LANES) % SHIFTS - EDGE
     phase = angle * freq[:, None] * lag[None, :]
     back = np.zeros((WIDE, LANES))
@@ -104,9 +105,17 @@
     return jnp.dot(a, b, preferred_element_type=F32)
 
 
-def thrice(x):
+def stacked(table, x):
     high, low = two(x)
-    return jnp.concatenate([high, low, high], axis=0)
+    count = table.shape[0] // 2
+    both = dot(table[...], high)
+    return both[:count] + both[count:] + dot(table[:count, :], low)
+
+
+def stacked_inner(table, x):
+    both = dot(table[...], jnp.concatenate(two(x), axis=0))
+    count = both.shape[0] // 2
+    return both[:count] + both[count:]
 
 
 def statistics(patch):
@@ -116,13 +125,24 @@
     return mean, lax.rsqrt(jnp.full((1, LANES), jnp.sum(centered * centered) / count + EPSILON))
 
 
-def spectra(inner, edge, mean, table, name, row):
-    core = dot(jnp.concatenate([inner, inner], axis=1), table["inner"][...])
-    rim = dot(jnp.concatenate([edge, edge], axis=1), table["edge_" + name][...])
+def across(inners, edges, table, name):
+    def twice(parts):
+        rows = jnp.concatenate(parts, axis=0)
+        return jnp.concatenate([rows, rows], axis=1)
+
+    core = dot(twice(inners), table["inner"][...])
+    rim = dot(twice(edges), table["edge_" + name][...])
+    return [
+        (core[n * SEARCH : (n + 1) * SEARCH], rim[n * SEARCH : (n + 1) * SEARCH])
+        for n in range(len(inners))
+    ]
+
+
+def spectra(core, rim, mean, table, name, row):
     sums = table["sums"]
     full = core + rim - mean * sums[row : row + 1, :]
     core = core[EDGE : EDGE + PATCH_SIDE] - mean * sums[0:1, :]
-    return dot(table["down_" + name][...], thrice(full)), dot(table["down_inner"][...], thrice(core))
+    return stacked(table["down_" + name], full), stacked_inner(table["down_inner"], core)
 
 
 def quarters(x):
@@ -292,60 +312,42 @@
         low, size = spans[q]
         return gathered.at[block, pl.ds(HALO + low, size), :]
 
-    def along_band(j, q, source):
-        to, there = (up, has_up) if q == 0 else (down, has_down)
-        copy = remote(source, halo(held[j], q), band_send.at[j, q], band_recv.at[j, q], to)
-        when(there, copy.start)
-        pending.append((there, copy.wait_send))
-
     up, down = (band - 1, strip), (band + 1, strip)
     to_mate = (band, pair)
 
-    def to_pair(j, q, source):
-        copy = remote(source, piece(held[j], q), pair_send.at[j, q], pair_recv.at[j, q], to_mate)
-        copy.start()
-        pending.append((None, copy.wait_send))
-        pending.append((None, copy.wait_recv))
-
-    arriving = {}
-
-    def in_plane(j, q, i, source):
-        new = j + (1 << i)
-        copy = remote(
-            source,
-            piece(held[j], q),
-            plane_send.at[new, q],
-            plane_recv.at[new, q],
-            (band, step(strip, i)),
-        )
-        copy.start()
-        pending.append((None, copy.wait_send))
-        arriving[new, q] = copy
-
-    for q, (low, size) in enumerate(spans):
-        source = second.at[pl.ds(low, size), :]
-        for i in range(len(bits)):
-            in_plane(0, q, i, source)
-        if q < 2:
-            along_band(0, q, source)
-        to_pair(0, q, source)
-
     for i in range(len(bits)):
         held += [step(value, i) for value in held]
-
-    order = []
-    for i in range(len(bits)):
-        group = [j for j in range(1, len(held)) if bin(j).count("1") == i + 1]
-        order += [(j, q) for q in range(len(spans)) for j in group]
+    sides = [(band, step(strip, i)) for i in range(len(bits))]
+    arriving, onward, leaving = {}, {}, []
+    for j in range(len(held)):
+        for q, (low, size) in enumerate(spans):
+            source = piece(held[j], q) if j else second.at[pl.ds(low, size), :]
+            after = []
+            for i in range(j.bit_length(), len(bits)):
+                new = j + (1 << i)
+                copy = remote(
+                    source, piece(held[j], q), plane_send.at[new, q], plane_recv.at[new, q], sides[i]
+                )
+                arriving[new, q] = copy
+                after.append((None, copy))
+            if q < 2:
+                to, there = (up, has_up) if q == 0 else (down, has_down)
+                copy = remote(source, halo(held[j], q), band_send.at[j, q], band_recv.at[j, q], to)
+                after.append((there, copy))
+            copy = remote(source, piece(held[j], q), pair_send.at[j, q], pair_recv.at[j, q], to_mate)
+            after.append((None, copy))
+            pending.append((None, copy.wait_recv))
+            onward[j, q] = after
+            pending += [(there, copy.wait_send) for there, copy in after]
 
     def forward(j, q):
-        arriving[j, q].wait_recv()
-        source = piece(held[j], q)
-        for i in range(j.bit_length(), len(bits)):
-            in_plane(j, q, i, source)
-        if q < 2:
-            along_band(j, q, source)
-        to_pair(j, q, source)
+        if j:
+            arriving[j, q].wait_recv()
+        for there, copy in onward[j, q]:
+            when(there, copy.start)
+
+    for q in range(len(spans)):
+        forward(0, q)
 
     for block in range(strips):
         for side in range(2):
@@ -379,22 +381,42 @@
         inner = wide[window, place_of(here + 1)]
         edge = jnp.where(halves, wide[window, place_of(here + 2)], wide[window, place_of(here)])
         mean, gain = statistics(inner[EDGE : EDGE + PATCH_SIDE].astype(F32))
-        full, inside = spectra(inner, edge, mean, table, "around", 2)
+        ((line, rim),) = across([inner], [edge], table, "around")
+        full, inside = spectra(line, rim, mean, table, "around", 2)
         around_ref[k] = full
         core_ref[k] = inside * gain[:, :1]
         for copy in results(k):
             copy.start()
+        for at in range(patch_count):
+            due = [x for x in order if plan[x] == at]
+            if due:
+
+                @pl.when(k == at)
+                def _():
+                    for j, q in due:
+                        forward(j, q)
+
         return carry
 
-    done = 0
-    steps = len(order)
-    groups = GROUPS
-    for g in range(groups):
-        lax.fori_loop(g * patch_count // groups, (g + 1) * patch_count // groups, around_one, 0)
-        upto = (g + 1) * steps // groups
-        for j, q in order[done:upto]:
+    order = [
+        (j, q)
+        for n in range(1, len(bits) + 1)
+        for q in range(len(spans))
+        for j in range(1, len(held))
+        if bin(j).count("1") == n
+    ]
+    plan = {}
+    for j, q in order:
+        if bin(j).count("1") == 1:
+            plan[j, q] = patch_count * (0, 1, 4, 8, 11)[q] // 16
+        elif bin(j).count("1") == 2 and q < 2:
+            plan[j, q] = patch_count * 14 // 16
+        else:
+            plan[j, q] = patch_count
+    lax.fori_loop(0, patch_count, around_one, 0)
+    for j, q in order:
+        if plan[j, q] == patch_count:
             forward(j, q)
-        done = upto
 
     for j in range(len(held)):
         for side, there in ((0, has_down), (1, has_up)):
@@ -464,6 +486,7 @@
     for copy in fetch(turn_id, slot):
         copy.wait()
 
+    inners, edges, found = [], [], []
     for n in range(each):
         k = turn_id * each + n
         place, row, base = place_of(k)
@@ -484,7 +507,14 @@
         inner = jnp.where(within, centre, side)
         edge = jnp.where(within, side, centre).astype(BF16)
         mean, gain = statistics(inner[EDGE : EDGE + PATCH_SIDE])
-        full, inside = spectra(inner.astype(BF16), edge, mean, table, "search", 1)
+        inners.append(inner.astype(BF16))
+        edges.append(edge)
+        found.append((mean, gain))
+
+    lines = []
+    for n, (line, rim) in enumerate(across(inners, edges, table, "search")):
+        mean, gain = found[n]
+        full, inside = spectra(line, rim, mean, table, "search", 1)
         inside = inside * gain[:, :1]
         a, b, c, d = [
             ahead + behind
@@ -493,13 +523,16 @@
         spectrum = jnp.concatenate(
             [jnp.concatenate([a, c], axis=1), jnp.concatenate([b, d], axis=1)], axis=0
         )
-        lines = dot(table["back_down"][...], thrice(spectrum))
-        high, low = two(lines)
-        surface = dot(jnp.concatenate([high, low, high], axis=1), table["back_across"][...])
-        scale = valid[k].astype(F32) / (2.0 * PATCH_SIDE * CYCLE * CYCLE)
-        surface_ref[pl.ds(pl.multiple_of(k * half, half), half), :] = (
-            jnp.where(halves, surface[:half], surface[half:]) * scale
-        )
+        scale = valid[turn_id * each + n].astype(F32) / (2.0 * PATCH_SIDE * CYCLE * CYCLE)
+        lines.append(stacked(table["back_down"], spectrum) * scale)
+
+    high, low = two(jnp.concatenate(lines, axis=0))
+    surface = dot(jnp.concatenate([high, low, high], axis=1), table["back_across"][...])
+    for n in range(each):
+        k = turn_id * each + n
+        even = surface[2 * n * half : (2 * n + 1) * half]
+        odd = surface[(2 * n + 1) * half : (2 * n + 2) * half]
+        surface_ref[pl.ds(pl.multiple_of(k * half, half), half), :] = jnp.where(halves, even, odd)
 
     @pl.when(turn_id == pl.num_programs(0) - 1)
     def _():
@@ -509,12 +542,39 @@
             ]
 
 
+def windows(owner, tile, offset, valid, gathered, around, core):
+    patch_count = tile.shape[0]
+    made = tables()
+    latter = [jnp.asarray(made[name]) for name in LATTER]
+    spectrum = around.shape
+    dma = pltpu.SemaphoreType.DMA
+    each = EACH
+    block = pl.BlockSpec((each,) + spectrum[1:], lambda k, *_: (k, 0, 0))
+    return pl.pallas_call(
+        functools.partial(correlate, gathered.shape[1]),
+        out_shape=jax.ShapeDtypeStruct((patch_count, SHIFTS * SHIFTS), F32),
+        grid_spec=pltpu.PrefetchScalarGridSpec(
+            num_scalar_prefetch=4,
+            grid=(patch_count // each,),
+            in_specs=[pl.BlockSpec(memory_space=pl.ANY), block, block]
+            + [pl.BlockSpec(c.shape, lambda k, *_: (0, 0)) for c in latter],
+            out_specs=pl.BlockSpec((patch_count, SHIFTS * SHIFTS), lambda k, *_: (0, 0)),
+            scratch_shapes=[
+                pltpu.VMEM((2, each, 3, ROWS, LANES), gathered.dtype),
+                pltpu.VMEM((each, ROWS, LANES), F32),
+                pltpu.VMEM((each, ROWS, LANES), F32),
+                pltpu.VMEM((patch_count * SHIFTS // 2, LANES), F32),
+                dma((2, each, 3)),
+            ],
+        ),
+    )(owner, tile, offset, valid, gathered, around, core, *latter)
+
+
 def on_device(bands, strips, first_scene, second_scene, owner_strip, target_tile, offsets, valid_mask):
     patch_count = target_tile.shape[-1]
     rows, cols = second_scene.shape
     made = tables()
     former = [jnp.asarray(made[name]) for name in FORMER]
-    latter = [jnp.asarray(made[name]) for name in LATTER]
     held = max(strips // 2, 1)
     dma = pltpu.SemaphoreType.DMA
     pieces = SPLIT + 2
@@ -551,26 +611,7 @@
         ],
         compiler_params=pltpu.CompilerParams(collective_id=0, has_side_effects=True),
     )(first_scene, second_scene, *former)
-    each = EACH
-    block = pl.BlockSpec((each,) + spectrum[1:], lambda k, *_: (k, 0, 0))
-    result = pl.pallas_call(
-        functools.partial(correlate, rows + 2 * HALO),
-        out_shape=jax.ShapeDtypeStruct((patch_count, SHIFTS * SHIFTS), F32),
-        grid_spec=pltpu.PrefetchScalarGridSpec(
-            num_scalar_prefetch=4,
-            grid=(patch_count // each,),
-            in_specs=[pl.BlockSpec(memory_space=pl.ANY), block, block]
-            + [pl.BlockSpec(c.shape, lambda k, *_: (0, 0)) for c in latter],
-            out_specs=pl.BlockSpec((patch_count, SHIFTS * SHIFTS), lambda k, *_: (0, 0)),
-            scratch_shapes=[
-                pltpu.VMEM((2, each, 3, ROWS, LANES), second_scene.dtype),
-                pltpu.VMEM((each, ROWS, LANES), F32),
-                pltpu.VMEM((each, ROWS, LANES), F32),
-                pltpu.VMEM((patch_count * SHIFTS // 2, LANES), F32),
-                dma((2, each, 3)),
-            ],
-        ),
-    )(
+    result = windows(
         owner_strip.reshape(patch_count),
         target_tile.reshape(patch_count),
         offsets.reshape(patch_count, 2).T,
@@ -578,7 +619,6 @@
         gathered,
         around,
         core,
-        *latter,
     )
     return result.reshape(1, 1, patch_count, SHIFTS * SHIFTS)
 

time: 48.8 us -> 44.8 us (0.918)
  Pallas kernels: 48.6 us -> 44.6 us
    pallas_call x1, Pallas kernels: 19.3 us -> 14.8 us  [windows(): pl.pallas_call(functools.partial(correlate, gathered.shape[1]), out_shape...]
    pallas_call x1, Pallas kernels: 29.3 us -> 29.8 us  [on_device(): pl.pallas_call(functools.partial(exchange, bands, strips), out_shape=(jax...]
where the time goes in v4:
time: 44.8 us; the launch traced here: 44.6 us
  Pallas kernels  44.6 us (100%)
    pallas_call x1, Pallas kernels, on_device(): pl.pallas_call(functools.partial(exchange, bands, strips), out_shape=(jax...  29.8 us
    pallas_call x1, Pallas kernels, windows(): pl.pallas_call(functools.partial(correlate, gathered.shape[1]), out_shape...  14.8 us

profile of v4, /device:TPU:0, one launch (start us, length us, event | category | flops | bytes accessed | tf_op | source)
XLA Modules:
  0.0 44.6 jit_solution(17902834223757139686)
XLA Ops:
  0.0 29.8 %shard_map.172 = (bf16[8,640,512]{2,1,0:T(8,128)(2,1)}, f32[16,192,256]{2,1,0:T(8,128)}, f32[16,192,256]{2,1,0:T(8,128)}) custom-call(bf16[512,512]{1,0:T(8,128)(2,1)} %first.1, bf16[512,512]{1,0:T(8,128)(2,1)} %second.1, bf16[256,256]{1,0:T(8,128)(2,1)} %constant.18.clone.refs_0_, bf16[256,256]{1,0:T(8,128)(2,1)} %constant.19.clone.refs_1_, ...), custom_call_target="tpu_custom_call" | custom-call | tf_op jit(solution)/shard_map/pallas_call | solution.py:582
  29.8 14.8 %shard_map.173 = f32[16,4096]{1,0:T(8,128)} custom-call(s32[16]{0:T(128)} %bitcast.8, s32[16]{0:T(128)} %bitcast.9, s32[2,16]{1,0:T(2,128)} %bitcast.7, s32[16]{0:T(128)} %bitcast.10, bf16[8,640,512]{2,1,0:T(8,128)(2,1)} %get-tuple-element.8.gathered, f32[16,192,256]{2,1,0:T(8,128)} %get-tuple-element.9.around_ref, ...), custom_call_target="tpu_custom_call" | custom-call | tf_op jit(solution)/shard_map/pallas_call | solution.py:553
